TPU v7x, 32 devices: a whole 2x2x4 slice. The times are simulated.
32 devices in a mesh: dp: 8 (over z, x), head: 4 (over y, core).
Axes of the slice: x: 2, y: 2, z: 4, core: 2. Of those that a mesh axis runs over, the one named last changes fastest.
Arguments:
- tokens: bfloat16 [8192, 768], P(('dp', 'head')), may hold values from -6 to 6
- cotangent: bfloat16 [8192, 768], P(('dp', 'head')), may hold values from -6 to 6
- segments: int32 [8, 1024], P('dp'), may hold values from -1 to 169, as said below
- attention_master: float32 [768, 3072], P('dp')
- feedforward_master: float32 [768, 6144], P('dp'), may hold values from -0.21875 to 0.21875
- vector_master: float32 [12, 768], P(None, 'dp')
- attention_moment: float32 [768, 3072], P('dp'), may hold values from -0.0024414062 to 0.0024414062
- feedforward_moment: float32 [768, 6144], P('dp'), may hold values from -0.0024414062 to 0.0024414062
- vector_moment: float32 [12, 768], P(None, 'dp'), may hold values from -0.0024414062 to 0.0024414062
- attention_second: float32 [768, 3072], P('dp'), may hold values from 1.4110135e-07 to 5.644054e-07
- feedforward_second: float32 [768, 6144], P('dp'), may hold values from 1.4110135e-07 to 5.644054e-07
- vector_second: float32 [12, 768], P(None, 'dp'), may hold values from 1.4110135e-07 to 5.644054e-07
- attention_teacher: float32 [768, 3072], P('dp'), may hold values from -0.21875 to 0.21875
- feedforward_teacher: float32 [768, 6144], P('dp'), may hold values from -0.21875 to 0.21875
- vector_teacher: float32 [12, 768], P(None, 'dp')
Outputs:
- block_output: bfloat16 [8192, 768], P(('dp', 'head'))
- input_gradient: float32 [8192, 768], P(('dp', 'head'))
- gradient_norm: float32 [], replicated
- new_attention_master: float32 [768, 3072], P('dp')
- new_feedforward_master: float32 [768, 6144], P('dp')
- new_vector_master: float32 [12, 768], P(None, 'dp')
- new_attention_moment: float32 [768, 3072], P('dp')
- new_feedforward_moment: float32 [768, 6144], P('dp')
- new_vector_moment: float32 [12, 768], P(None, 'dp')
- new_attention_second: float32 [768, 3072], P('dp')
- new_feedforward_second: float32 [768, 6144], P('dp')
- new_vector_second: float32 [12, 768], P(None, 'dp')
- new_attention_teacher: float32 [768, 3072], P('dp')
- new_feedforward_teacher: float32 [768, 6144], P('dp')
- new_vector_teacher: float32 [12, 768], P(None, 'dp')
- attention_copy: bfloat16 [768, 3072], P('dp')
- feedforward_copy: bfloat16 [768, 6144], P('dp')
- vector_copy: bfloat16 [12, 768], P(None, 'dp')
Inputs may be any that keep to these rules, and one draw needn't show every extreme that they name: `segments`: in each pack, segment numbers start at 0 and rise by one from image to image; an image holds 2 + p * p tokens for some p from 2 to 12; -1 marks padding at the end of the pack, one token of it or more. In every draw one pack holds only images of 2 x 2 patches, as many as fit, so that its last image number is the largest possible.
All inputs are finite; a program needn't handle non-finite values.
Results may differ from a plain program's by a relative error of at most 0.012.
The roundings to bfloat16 on the way count: a program that leaves them out, or rounds other values in their place, can miss the bound.
Values may be sent and summed in bfloat16 or wider, within the bound.
No kernel may reach another device: no remote copies, remote signals or barrier semaphores. Data moves between devices by JAX's collectives and lax.ppermute only.
A program may use at most 192 MiB of HBM per device.

v0:
```python
import jax
import jax.numpy as jnp
from jax import lax
from jax.sharding import PartitionSpec as P

HEADS = 12
HEAD_DIM = 64
ADAM_STEP = 3


norm_epsilon = 1e-06
beta_one = 0.5
beta_two = 0.5
adam_epsilon = 1e-08
learn_rate = 0.05
weight_decay = 0.05
teacher_keep = 0.8
clip_limit = 1.0
masked_score = -1e30


def layer_norm(values, gain, shift):
    center = jnp.mean(values, axis=-1, keepdims=True)
    deviate = values - center
    spread = jnp.mean(deviate * deviate, axis=-1, keepdims=True)
    return deviate * lax.rsqrt(spread + norm_epsilon) * gain + shift


def gelu_exact(values):
    return 0.5 * values * (1.0 + lax.erf(values * 0.7071067811865476))


def adam_update(master, moment, second, teacher, gradient, factor, decay_rate):
    clipped = gradient * factor
    moment_new = beta_one * moment + (1.0 - beta_one) * clipped
    second_new = beta_two * second + (1.0 - beta_two) * clipped * clipped
    scale_one = 1.0 - beta_one**ADAM_STEP
    scale_two = 1.0 - beta_two**ADAM_STEP
    update = moment_new / scale_one / (jnp.sqrt(second_new / scale_two) + adam_epsilon)
    master_new = master * (1.0 - learn_rate * decay_rate) - learn_rate * update
    teacher_new = teacher_keep * teacher + (1.0 - teacher_keep) * master_new
    return (master_new, moment_new, second_new, teacher_new)


def contract_rows(left, right):
    return lax.dot_general(
        left, right, (((0,), (0,)), ((), ())), preferred_element_type=jnp.float32
    )


def contract_cols(left, right):
    return lax.dot_general(
        left, right, (((1,), (1,)), ((), ())), preferred_element_type=jnp.float32
    )


def to_items(array, seq_count, per_device):
    shaped = array.reshape(seq_count, -1, per_device, HEAD_DIM).transpose(0, 2, 1, 3)
    return shaped.reshape(seq_count * per_device, -1, HEAD_DIM)


def from_items(array, seq_count, per_device):
    shaped = array.reshape(seq_count, per_device, -1, HEAD_DIM).transpose(0, 2, 1, 3)
    return shaped.reshape(-1, 1, per_device * HEAD_DIM)


def masked_scores(queries, key_rows, segment_ids):
    raw_score = contract_cols(queries, key_rows) * HEAD_DIM ** (-0.5)
    same_image = segment_ids[:, None] == segment_ids[None, :]
    return jnp.where(same_image, raw_score, masked_score)


def attend_packed(packed):
    queries, key_rows, value_rows, segment_ids = packed
    scores = masked_scores(queries, key_rows, segment_ids)
    largest = jnp.max(scores, axis=-1, keepdims=True)
    log_total = largest + jnp.log(jnp.sum(jnp.exp(scores - largest), axis=-1, keepdims=True))
    attention = jnp.exp(scores - log_total).astype(jnp.bfloat16)
    attended = jnp.dot(attention, value_rows, preferred_element_type=jnp.float32)
    return (attended.astype(jnp.bfloat16), log_total[:, 0])


def attend_back_packed(packed):
    queries, key_rows, value_rows, segment_ids, log_total, grad_out = packed
    scores = masked_scores(queries, key_rows, segment_ids)
    attention = jnp.exp(scores - log_total[:, None])
    grad_attention = contract_cols(grad_out, value_rows)
    grad_scores = attention * (
        grad_attention - jnp.sum(attention * grad_attention, axis=-1, keepdims=True)
    )
    grad_low = grad_scores.astype(jnp.bfloat16)
    score_scale = HEAD_DIM ** (-0.5)
    grad_query = score_scale * jnp.dot(grad_low, key_rows, preferred_element_type=jnp.float32)
    grad_key = score_scale * contract_rows(grad_low, queries)
    grad_value = contract_rows(attention.astype(jnp.bfloat16), grad_out)
    return (
        grad_query.astype(jnp.bfloat16),
        grad_key.astype(jnp.bfloat16),
        grad_value.astype(jnp.bfloat16),
    )


def split_groups(attention_part, forward_part, vector_part, width, hidden):
    return [
        attention_part[:, : 3 * width],
        attention_part[:, 3 * width :],
        forward_part[:, :hidden],
        forward_part[:, hidden:],
        vector_part,
    ]


def local(
    tokens,
    cotangent,
    segments,
    attention_master,
    feedforward_master,
    vector_master,
    attention_moment,
    feedforward_moment,
    vector_moment,
    attention_second,
    feedforward_second,
    vector_second,
    attention_teacher,
    feedforward_teacher,
    vector_teacher,
):
    width = tokens.shape[1]
    rows_local = tokens.shape[0]
    groups = lax.axis_size("head")
    hidden = feedforward_master.shape[1] // 2
    seq_count = segments.shape[0]
    per_device = HEADS // groups
    head_cols = per_device * HEAD_DIM
    attention_low, forward_low, vector_low = (
        lax.all_gather(attention_master.astype(jnp.bfloat16), "dp", axis=0, tiled=True),
        lax.all_gather(feedforward_master.astype(jnp.bfloat16), "dp", axis=0, tiled=True),
        lax.all_gather(vector_master.astype(jnp.bfloat16), "dp", axis=1, tiled=True),
    )
    vector_full = vector_low.astype(jnp.float32)
    norm_gain = vector_full[0]
    norm_shift = vector_full[1]
    query_bias = vector_full[2]
    value_bias = vector_full[3]
    output_bias = vector_full[4]
    second_gain = vector_full[5]
    second_shift = vector_full[6]
    down_bias = vector_full[7]
    up_bias = vector_full[8:12].reshape(-1)
    w_qkv = attention_low[:, : 3 * width]
    w_out = attention_low[:, 3 * width :]
    w_up = forward_low[:, :hidden]
    w_down = forward_low[:, hidden:]
    inputs = tokens.astype(jnp.float32)
    normed = layer_norm(inputs, norm_gain, norm_shift).astype(jnp.bfloat16)
    qkv_bias = jnp.concatenate([query_bias, jnp.zeros_like(query_bias), value_bias])
    projected = (jnp.dot(normed, w_qkv, preferred_element_type=jnp.float32) + qkv_bias).astype(
        jnp.bfloat16
    )
    projected = projected.reshape(rows_local, 3, groups, head_cols)
    heads_query, heads_key, heads_value = (
        lax.all_to_all(projected[:, 0], "head", split_axis=1, concat_axis=0, tiled=True),
        lax.all_to_all(projected[:, 1], "head", split_axis=1, concat_axis=0, tiled=True),
        lax.all_to_all(projected[:, 2], "head", split_axis=1, concat_axis=0, tiled=True),
    )
    query_items = to_items(heads_query, seq_count, per_device)
    key_items = to_items(heads_key, seq_count, per_device)
    value_items = to_items(heads_value, seq_count, per_device)
    segment_items = jnp.repeat(segments, per_device, axis=0)
    attended, log_totals = lax.map(
        attend_packed, (query_items, key_items, value_items, segment_items)
    )
    back_tokens = lax.all_to_all(
        from_items(attended, seq_count, per_device), "head", split_axis=0, concat_axis=1, tiled=True
    )
    mixed_rows = back_tokens.reshape(rows_local, width)
    resid = inputs + jnp.dot(mixed_rows, w_out, preferred_element_type=jnp.float32) + output_bias
    normed_two = layer_norm(resid, second_gain, second_shift).astype(jnp.bfloat16)
    pre_act = jnp.dot(normed_two, w_up, preferred_element_type=jnp.float32) + up_bias
    activated = gelu_exact(pre_act).astype(jnp.bfloat16)
    branch_out = contract_cols(activated, w_down) + down_bias
    block_output = (resid + branch_out).astype(jnp.bfloat16)
    grad_output = cotangent.astype(jnp.float32)
    grad_down = contract_rows(cotangent, activated)
    grad_down_bias = jnp.sum(grad_output, axis=0)
    grad_act = jnp.dot(cotangent, w_down, preferred_element_type=jnp.float32)
    _, gelu_pull = jax.vjp(gelu_exact, pre_act)
    grad_pre = gelu_pull(grad_act)[0].astype(jnp.bfloat16)
    grad_up = contract_rows(normed_two, grad_pre)
    grad_up_bias = jnp.sum(grad_pre.astype(jnp.float32), axis=0)
    grad_normed_two = contract_cols(grad_pre, w_up)
    _, norm_pull_two = jax.vjp(layer_norm, resid, second_gain, second_shift)
    grad_resid_norm, grad_second_gain, grad_second_shift = norm_pull_two(grad_normed_two)
    grad_resid = grad_output + grad_resid_norm
    grad_branch = grad_resid.astype(jnp.bfloat16)
    grad_out_weight = contract_rows(mixed_rows, grad_branch)
    grad_out_bias = jnp.sum(grad_branch.astype(jnp.float32), axis=0)
    grad_mixed = (
        contract_cols(grad_branch, w_out)
        .astype(jnp.bfloat16)
        .reshape(rows_local, groups, head_cols)
    )
    heads_grad = lax.all_to_all(grad_mixed, "head", split_axis=1, concat_axis=0, tiled=True)
    grad_items = to_items(heads_grad, seq_count, per_device)
    query_grads, key_grads, value_grads = lax.map(
        attend_back_packed,
        (query_items, key_items, value_items, segment_items, log_totals, grad_items),
    )
    grad_query, grad_key, grad_value = (
        lax.all_to_all(
            from_items(query_grads, seq_count, per_device),
            "head",
            split_axis=0,
            concat_axis=1,
            tiled=True,
        ),
        lax.all_to_all(
            from_items(key_grads, seq_count, per_device),
            "head",
            split_axis=0,
            concat_axis=1,
            tiled=True,
        ),
        lax.all_to_all(
            from_items(value_grads, seq_count, per_device),
            "head",
            split_axis=0,
            concat_axis=1,
            tiled=True,
        ),
    )
    grad_query = grad_query.reshape(rows_local, width)
    grad_key = grad_key.reshape(rows_local, width)
    grad_value = grad_value.reshape(rows_local, width)
    grad_qkv = jnp.concatenate([grad_query, grad_key, grad_value], axis=1)
    grad_qkv_weight = contract_rows(normed, grad_qkv)
    grad_query_bias = jnp.sum(grad_query.astype(jnp.float32), axis=0)
    grad_value_bias = jnp.sum(grad_value.astype(jnp.float32), axis=0)
    grad_normed = contract_cols(grad_qkv, w_qkv)
    _, norm_pull = jax.vjp(layer_norm, inputs, norm_gain, norm_shift)
    grad_in_norm, grad_norm_gain, grad_norm_shift = norm_pull(grad_normed)
    input_gradient = grad_resid + grad_in_norm
    grad_vector = jnp.concatenate(
        [
            jnp.stack(
                [
                    grad_norm_gain,
                    grad_norm_shift,
                    grad_query_bias,
                    grad_value_bias,
                    grad_out_bias,
                    grad_second_gain,
                    grad_second_shift,
                    grad_down_bias,
                ]
            ),
            grad_up_bias.reshape(4, width),
        ],
        axis=0,
    )
    masters = split_groups(attention_master, feedforward_master, vector_master, width, hidden)
    moments = split_groups(attention_moment, feedforward_moment, vector_moment, width, hidden)
    seconds = split_groups(attention_second, feedforward_second, vector_second, width, hidden)
    teachers = split_groups(attention_teacher, feedforward_teacher, vector_teacher, width, hidden)
    decays = [weight_decay, weight_decay, weight_decay, weight_decay, 0.0]
    owned = (
        lax.psum_scatter(grad_qkv_weight, "dp", scatter_dimension=0, tiled=True),
        lax.psum_scatter(grad_out_weight, "dp", scatter_dimension=0, tiled=True),
        lax.psum_scatter(grad_up, "dp", scatter_dimension=0, tiled=True),
        lax.psum_scatter(grad_down, "dp", scatter_dimension=0, tiled=True),
        lax.psum_scatter(grad_vector, "dp", scatter_dimension=1, tiled=True),
    )
    shards = lax.psum((owned[0], owned[1], owned[2], owned[3], owned[4]), "head")
    squares = (
        jnp.sum(shards[0] * shards[0])
        + jnp.sum(shards[1] * shards[1])
        + jnp.sum(shards[2] * shards[2])
        + jnp.sum(shards[3] * shards[3])
        + jnp.sum(shards[4] * shards[4])
    )
    total = lax.psum(squares, "dp")
    gradient_norm = jnp.sqrt(total)
    factor = jnp.minimum(1.0, clip_limit / (gradient_norm + 1e-06))
    results = []
    for member in range(5):
        results.append(
            adam_update(
                masters[member],
                moments[member],
                seconds[member],
                teachers[member],
                shards[member],
                factor,
                decays[member],
            )
        )
    joined = []
    for state in range(4):
        joined.append(
            (
                jnp.concatenate([results[0][state], results[1][state]], axis=1),
                jnp.concatenate([results[2][state], results[3][state]], axis=1),
                results[4][state],
            )
        )
    return (
        block_output,
        input_gradient,
        gradient_norm,
        joined[0][0],
        joined[0][1],
        joined[0][2],
        joined[1][0],
        joined[1][1],
        joined[1][2],
        joined[2][0],
        joined[2][1],
        joined[2][2],
        joined[3][0],
        joined[3][1],
        joined[3][2],
        joined[0][0].astype(jnp.bfloat16),
        joined[0][1].astype(jnp.bfloat16),
        joined[0][2].astype(jnp.bfloat16),
    )


def solution(mesh):
    placed = (
        P(("dp", "head"), None),
        P(("dp", "head"), None),
        P("dp", None),
        P("dp", None),
        P("dp", None),
        P(None, "dp"),
        P("dp", None),
        P("dp", None),
        P(None, "dp"),
        P("dp", None),
        P("dp", None),
        P(None, "dp"),
        P("dp", None),
        P("dp", None),
        P(None, "dp"),
    )
    return jax.shard_map(
        local,
        mesh=mesh,
        in_specs=placed,
        out_specs=(
            P(("dp", "head"), None),
            P(("dp", "head"), None),
            P(),
            P("dp", None),
            P("dp", None),
            P(None, "dp"),
            P("dp", None),
            P("dp", None),
            P(None, "dp"),
            P("dp", None),
            P("dp", None),
            P(None, "dp"),
            P("dp", None),
            P("dp", None),
            P(None, "dp"),
            P("dp", None),
            P("dp", None),
            P(None, "dp"),
        ),
        check_vma=False,
    )
```

profile of v0, /device:TPU:0, one launch (start us, length us, event | category | flops | bytes accessed | tf_op | source)
XLA Modules:
  0.0 1002.0 jit_solution(6333419613768057943)
XLA Ops:
  7.2 2.2 convert_element_type.90
  9.5 2.9 convert_element_type.93
  12.4 32.5 %all-gather = bf16[8,96,12]{1,2,0:T(8,128)(2,1)S(1)} all-gather(bf16[1,96,12]{1,2,0:T(8,128)(2,1)S(1)} %convert_bitcast_fusion), channel_id=1, replica_groups=mesh['dp'=8,'head'=4] {'dp'}, dimensions={0}, use_global_device_ids=true | all-gather | bytes 20736 | tf_op jit(solution)/shard_map/all_gather | solution.py:140
  46.1 47.5 %all-gather.4.cloned.1.call-done = bf16[768,3072]{1,0:T(8,128)(2,1)} async-done(((bf16[96,3072]{1,0:T(8,128)(2,1)}), bf16[768,3072]{1,0:T(8,128)(2,1)}) %all-gather.4.cloned.1.call-update) | async-done | bytes 4718608 | tf_op jit(solution)/shard_map/all_gather | solution.py:138
  93.6 3.2 fusion.64
  98.3 10.0 all_to_all.120
  108.2 9.8 all_to_all.121
  118.1 3.5 all-to-all-start
  122.7 6.2 all-to-all-done
  131.4 13.1 %while.26 = (s32[]{:T(128)}, bf16[3,1024,64]{1,2,0:T(8,128)(2,1)S(1)}, f32[3,1024]{1,0:T(4,128)}, s32[3,1024]{1,0:T(4,128)S(1)}, bf16[3,1024,64]{2,1,0:T(8,128)(...) while((s32[]{:T(128)}, ...), condition=%wide.region_5.6_spmd, body=%wide.region_2.5_spmd.sunk | while | flops 283180032 | bytes 13568109 | solution.py:172
  134.4 1.4 dynamic_update_slice.27
  145.1 1.7 reduce.20
  147.9 1.4 reshape.269
  149.3 3.7 all-to-all-start.3
  154.3 6.0 all-to-all-done.3
  160.4 1.9 reshape.270
  162.3 2.3 copy.133
  165.0 2.0 fusion.119
  167.3 65.3 %all-gather.6.cloned.1.call-done = bf16[768,6144]{1,0:T(8,128)(2,1)} async-done(((bf16[96,6144]{1,0:T(8,128)(2,1)}), bf16[768,6144]{1,0:T(8,128)(2,1)}) %all-gather.6.cloned.1.call-update) | async-done | bytes 9437200 | tf_op jit(solution)/shard_map/all_gather | solution.py:139
  232.6 5.4 multiply_convert_fusion.1
  238.0 3.5 convert_reduce_fusion
  241.5 2.1 multiply_reduce_fusion.4
  246.2 1.8 convolution_convert_fusion
  248.9 3.5 all-to-all-start.4
  252.6 2.9 fusion.120
  255.5 4.2 all-to-all-done.4
  263.7 27.2 %while.27 = (s32[]{:T(128)}, bf16[3,1024,64]{1,2,0:T(8,128)(2,1)}, bf16[3,1024,64]{1,2,0:T(8,128)(2,1)}, bf16[3,1024,64]{1,2,0:T(8,128)(2,1)S(1)}, s32[3,1024]{1...) while((s32[]{:T(128)}, bf16[3,1024,64]{1,2,0:T(8,128)(2,1)}, ...), condition=%wide.region_12.13_spmd, body=%wide.region_10.12_spmd.sunk | while | flops 681901056 | bytes 36611252 | solution.py:207
  265.2 1.6 fusion.159
  270.1 1.4 fusion.161
  274.3 1.6 fusion.159
  279.2 1.4 fusion.161
  283.3 1.6 fusion.159
  288.2 1.4 fusion.161
  291.0 1.9 reduce.23
  293.1 1.4 reshape.275
  294.4 3.5 all-to-all-start.5
  300.4 4.9 all-to-all-done.5
  305.3 3.5 all-to-all-start.7
  308.8 2.0 reduce.22
  312.3 3.9 all-to-all-done.7
  316.2 3.5 all-to-all-start.6
  320.5 1.7 copy.148
  325.0 1.7 copy.142
  330.6 5.4 fusion.97
  337.2 6.7 fusion.107
  344.9 6.6 convolution_bitcast_fusion
  358.6 3.5 fusion.108
  365.1 98.8 %reduce-scatter.8.cloned.1.call-done = f32[96,2304]{1,0:T(8,128)} async-done(((f32[768,2304]{1,0:T(8,128)}), f32[96,2304]{1,0:T(8,128)}) %reduce-scatter.8.cloned.1.call-update) | async-done | bytes 884752 | tf_op jit(solution)/shard_map/reduce_scatter | solution.py:269
  463.9 166.4 %reduce-scatter.12.cloned.1.call-done = f32[96,3072]{1,0:T(8,128)} async-done(((f32[768,3072]{1,0:T(8,128)}), f32[96,3072]{1,0:T(8,128)}) %reduce-scatter.12.cloned.1.call-update) | async-done | bytes 1179664 | tf_op jit(solution)/shard_map/reduce_scatter | solution.py:271
  630.3 166.4 %reduce-scatter.14.cloned.1.call-done = f32[96,3072]{1,0:T(8,128)} async-done(((f32[768,3072]{1,0:T(8,128)}), f32[96,3072]{1,0:T(8,128)}) %reduce-scatter.14.cloned.1.call-update) | async-done | bytes 1179664 | tf_op jit(solution)/shard_map/reduce_scatter | solution.py:272
  796.8 64.7 %reduce-scatter.16.cloned.1.call-done = f32[96,12]{1,0:T(8,128)} async-done(((f32[768,12]{1,0:T(8,128)}), f32[96,12]{1,0:T(8,128)}) %reduce-scatter.16.cloned.1.call-update) | async-done | bytes 4624
  862.4 5.8 psum.46
  868.7 70.0 %all-reduce.3.cloned.1.call-done = (f32[96,2304]{1,0:T(8,128)}, f32[96,768]{1,0:T(8,128)}, f32[96,3072]{1,0:T(8,128)}, f32[96,3072]{1,0:T(8,128)}) async-done(((f32[96,2304]{1,0:T(8,128)}, f32[96,768]{1,0:T(8,128)}, f32[96,3072]{1,0:T(8,128)}, f32[96,3072]{1,0:T(8,128)}), (f32[96,2304]{1,0:T(8,128)}, f32[96,768]{1,0:T(8,128)}, f32[96,3072]{1,0:T(8,128)}, f32[96,3072]{1,0:T(8,128)})) %all-reduce.3.cloned.1.call-update) | async-done | bytes 3538960 | tf_op jit(solution)/shard_map/psum | solution.py:275
  938.7 2.3 multiply_reduce_fusion.1
  941.0 2.2 multiply_reduce_fusion.2
  948.0 5.1 fusion.77
  953.0 22.0 %psum.47 = f32[]{:T(128)} all-reduce(f32[]{:T(128)S(6)} %add.253), channel_id=1, replica_groups=mesh['dp'=8,'head'=4] {'dp'}, use_global_device_ids=true, to_apply=%region_39.40 | all-reduce | flops 1 | bytes 8 | tf_op jit(solution)/shard_map/psum | solution.py:283
  975.8 1.6 multiply_add_fusion.7
  977.4 2.6 multiply_add_fusion.5
  981.4 3.2 multiply_add_fusion.4
  984.6 1.8 fusion.112
  986.4 1.7 pad_maximum_fusion.6
  988.0 2.9 fusion.111
  990.9 2.6 pad_maximum_fusion.1
  (247 shorter events, 75.3 us)
Async XLA Ops:
  7.2 86.4 %all-gather.4.cloned.1.call-start = ((), (), s32[]{:S(2)}) async-start(), calls=%async_computation.13 | async-start | bytes 5308416 | tf_op jit(solution)/shard_map/all_gather | solution.py:138
  9.4 3.0 copy-start.29
  9.4 36.2 %copy-start = (bf16[256,768]{1,0:T(8,128)(2,1)S(1)}, bf16[256,768]{1,0:T(8,128)(2,1)}, u32[]{:S(2)}) copy-start(bf16[256,768]{1,0:T(8,128)(2,1)} %param.19) | copy-start | bytes 1179652
  9.4 223.1 %all-gather.6.cloned.1.call-start = ((), (), s32[]{:S(2)}) async-start(), calls=%async_computation.14 | async-start | bytes 10616832 | tf_op jit(solution)/shard_map/all_gather | solution.py:139
  45.0 51.8 %copy-start.24 = (f32[768,12]{0,1:T(8,128)}, f32[768,12]{0,1:T(8,128)S(1)}, u32[]{:S(2)}) copy-start(f32[768,12]{0,1:T(8,128)S(1)} %reshape.258) | copy-start | bytes 110596
  45.8 51.0 %copy-start.25 = (f32[256]{0:T(256)}, f32[256]{0:T(256)S(1)}, u32[]{:S(2)}) copy-start(f32[256]{0:T(256)S(1)} %broadcast_multiply_fusion.1) | copy-start | bytes 3076
  46.1 50.7 %copy-start.42 = (f32[256]{0:T(256)}, f32[256]{0:T(256)S(1)}, u32[]{:S(2)}) copy-start(f32[256]{0:T(256)S(1)} %fusion.94) | copy-start | bytes 3076
  46.1 50.7 %copy-start.31 = (f32[256]{0:T(256)}, f32[256]{0:T(256)S(1)}, u32[]{:S(2)}) copy-start(f32[256]{0:T(256)S(1)} %fusion.100) | copy-start | bytes 3076
  118.1 10.9 %all-to-all-start = ((bf16[256,4,192]{0,2,1:T(8,128)(2,1)}), bf16[256,4,192]{0,2,1:T(8,128)(2,1)S(1)}, u32[]{:S(2)}, u32[]{:S(2)}) async-start(bf16[256,4,192]{0,2,1:T(8,128)(2,1)} %get-tuple-element.291), calls=%async_computation | async-start | bytes 786432 | tf_op jit(solution)/shard_map/all_to_all | solution.py:164
  144.5 17.8 %copy-start.4 = (bf16[3,1024,64]{2,1,0:T(8,128)(2,1)}, bf16[3,1024,64]{2,1,0:T(8,128)(2,1)S(1)}, u32[]{:S(2)}) copy-start(bf16[3,1024,64]{2,1,0:T(8,128)(2,1)S(1)} %get-tuple-element.505) | copy-start | bytes 1179652
  149.3 11.1 %all-to-all-start.3 = ((bf16[4,2,24576]{2,1,0:T(2,128)(2,1)}), bf16[4,2,24576]{2,1,0:T(2,128)(2,1)S(1)}, u32[]{:S(2)}, u32[]{:S(2)}) async-start(bf16[4,2,24576]{2,1,0:T(2,128)(2,1)} %reshape.269), calls=%async_computation.3 | async-start | bytes 786432 | tf_op jit(solution)/shard_map/all_to_all | solution.py:175
  165.0 73.1 %copy-start.14 = (bf16[256,4,1,192]{0,3,1,2:T(8,128)(2,1)}, bf16[256,4,1,192]{0,3,1,2:T(8,128)(2,1)S(1)}, u32[]{:S(2)}) copy-start(bf16[256,4,1,192]{0,3,1,2:T(8,128)(2,1)S(1)} %copy.134) | copy-start | bytes 1179652
  165.0 67.6 %copy-start.41 = (f32[3072]{0:T(1024)S(1)}, f32[3072]{0:T(1024)}, u32[]{:S(2)}) copy-start(f32[3072]{0:T(1024)} %add.240) | copy-start | bytes 36868
  167.0 76.6 %copy-start.2 = (f32[256,768]{1,0:T(8,128)}, f32[256,768]{1,0:T(8,128)S(1)}, u32[]{:S(2)}) copy-start(f32[256,768]{1,0:T(8,128)S(1)} %get-tuple-element.295) | copy-start | bytes 2359300
  167.0 74.5 %copy-start.34 = (f32[256]{0:T(256)}, f32[256]{0:T(256)S(1)}, u32[]{:S(2)}) copy-start(f32[256]{0:T(256)S(1)} %broadcast_multiply_fusion) | copy-start | bytes 3076
  167.3 74.2 %copy-start.36 = (f32[256]{0:T(256)}, f32[256]{0:T(256)S(1)}, u32[]{:S(2)}) copy-start(f32[256]{0:T(256)S(1)} %fusion.101) | copy-start | bytes 3076
  232.6 5.4 copy-start.8
  232.6 5.4 copy-start.50
  241.5 2.1 copy-start.19
  244.7 0.8 copy-start.44
  245.5 7.2 copy-start.15
  248.9 10.9 %all-to-all-start.4 = ((bf16[256,4,192]{0,2,1:T(8,128)(2,1)}), bf16[256,4,192]{0,2,1:T(8,128)(2,1)S(1)}, u32[]{:S(2)}, u32[]{:S(2)}) async-start(bf16[256,4,192]{0,2,1:T(8,128)(2,1)} %bitcast.208), calls=%async_computation.4 | async-start | bytes 786432 | tf_op jit(solution)/shard_map/all_to_all | solution.py:205
  252.4 112.7 %reduce-scatter.10.cloned.1.call-start = ((), (), s32[]{:S(2)}) async-start(), calls=%async_computation.16 | async-start | bytes 2654208 | tf_op jit(solution)/shard_map/reduce_scatter | solution.py:270
  270.1 1.4 copy-start.17
  279.1 1.4 copy-start.17
  288.2 1.4 copy-start.17
  294.4 10.9 %all-to-all-start.5 = ((bf16[4,2,24576]{2,1,0:T(2,128)(2,1)}), bf16[4,2,24576]{2,1,0:T(2,128)(2,1)S(1)}, u32[]{:S(2)}, u32[]{:S(2)}) async-start(bf16[4,2,24576]{2,1,0:T(2,128)(2,1)} %reshape.275), calls=%async_computation.5 | async-start | bytes 786432 | tf_op jit(solution)/shard_map/all_to_all | solution.py:212
  305.3 10.9 %all-to-all-start.7 = ((bf16[4,2,24576]{2,1,0:T(2,128)(2,1)}), bf16[4,2,24576]{2,1,0:T(2,128)(2,1)S(1)}, u32[]{:S(2)}, u32[]{:S(2)}) async-start(bf16[4,2,24576]{2,1,0:T(2,128)(2,1)} %reshape.271), calls=%async_computation.7 | async-start | bytes 786432 | tf_op jit(solution)/shard_map/all_to_all | solution.py:226
  316.2 12.7 %all-to-all-start.6 = ((bf16[4,2,24576]{2,1,0:T(2,128)(2,1)}), bf16[4,2,24576]{2,1,0:T(2,128)(2,1)S(1)}, u32[]{:S(2)}, u32[]{:S(2)}) async-start(bf16[4,2,24576]{2,1,0:T(2,128)(2,1)} %reshape.273), calls=%async_computation.6 | async-start | bytes 786432 | tf_op jit(solution)/shard_map/all_to_all | solution.py:219
  319.7 144.2 %reduce-scatter.8.cloned.1.call-start = ((), (), s32[]{:S(2)}) async-start(), calls=%async_computation.15 | async-start | bytes 7962624 | tf_op jit(solution)/shard_map/reduce_scatter | solution.py:269
  328.9 1.7 copy-start.26
  328.9 1.7 copy-start.32
  330.6 5.4 copy-start.21
  336.0 1.1 copy-start.3
  336.0 1.1 copy-start.35
  336.0 1.1 copy-start.37
  336.1 294.3 %reduce-scatter.12.cloned.1.call-start = ((), (), s32[]{:S(2)}) async-start(), calls=%async_computation.17 | async-start | bytes 10616832 | tf_op jit(solution)/shard_map/reduce_scatter | solution.py:271
  343.9 1.0 copy-start.9
  343.9 452.8 %reduce-scatter.14.cloned.1.call-start = ((), (), s32[]{:S(2)}) async-start(), calls=%async_computation.18 | async-start | bytes 10616832 | tf_op jit(solution)/shard_map/reduce_scatter | solution.py:272
  351.5 7.1 copy-start.20
  351.5 510.0 %reduce-scatter.16.cloned.1.call-start = ((), (), s32[]{:S(2)}) async-start(), calls=%async_computation.19 | async-start | bytes 442368
  358.5 3.6 copy-start.43
  358.5 3.6 copy-start.27
  358.6 3.6 copy-start.33
  358.6 4.1 copy-start.45
  362.1 1.9 copy-start.38
  362.1 1.9 copy-start.39
  362.1 1.9 copy-start.40
  365.0 573.7 %all-reduce.3.cloned.1.call-start = ((), (), s32[]{:S(2)}) async-start(), calls=%async_computation.20 | async-start | bytes 7077888 | tf_op jit(solution)/shard_map/psum | solution.py:275
  796.8 151.1 %copy-start.49 = (f32[768]{0:T(1024)S(1)}, f32[768]{0:T(1024)}, u32[]{:S(2)}) copy-start(f32[768]{0:T(1024)} %get-tuple-element.207) | copy-start | bytes 9220
  938.7 4.5 copy-start.22
  938.7 5.1 copy-start.10
  947.9 27.8 %copy-start.7 = (f32[96,3072]{1,0:T(8,128)S(1)}, f32[96,3072]{1,0:T(8,128)}, u32[]{:S(2)}) copy-start(f32[96,3072]{1,0:T(8,128)} %param.22) | copy-start | bytes 3538948
  953.0 24.3 %copy-start.11 = (f32[96,2304]{1,0:T(8,128)S(1)}, f32[96,2304]{1,0:T(8,128)}, u32[]{:S(2)}) copy-start(f32[96,2304]{1,0:T(8,128)} %get-tuple-element.249) | copy-start | bytes 2654212
  975.8 5.5 copy-start.13
  977.4 2.7 copy-start.30
  977.4 2.7 copy-start.46
  977.4 2.7 copy-start.47
  977.4 3.3 copy-start.48
  977.4 3.9 copy-start.1
  977.4 3.9 copy-start.5
  977.4 3.9 copy-start.6
  977.4 3.9 copy-start.12
  980.7 3.9 copy-start.28
  (5 other events, 3.6 us)
Sparse Core Ops, SparseCore 0:
  10.8 82.7 all-gather.3
  96.3 136.1 all-gather.5
  257.3 67.7 reduce-scatter.9
  336.2 127.6 reduce-scatter.7
  467.8 162.5 reduce-scatter.11
  634.2 162.5 reduce-scatter.13
  800.9 60.4 reduce-scatter.15
  864.3 74.4 all-reduce.2
where the time goes:
time: 1010 us; the launch traced here: 1000 us
  waiting for transfers between devices  705 us (70%)
  blocking collectives  80.1 us (8%)
  matrix products  71 us (7%)
  local copies, waits for them, and re-layouts  56.3 us (6%)
  other arithmetic  47.5 us (5%)
  starting transfers between devices  21.8 us (2%)
  between operations  20.5 us (2%)
    reduce_scatter x1, waiting for transfers between devices, local(): lax.psum_scatter(grad_down, 'dp', scatter_dimension=0, tiled=True)  166 us
    reduce_scatter x1, waiting for transfers between devices, local(): lax.psum_scatter(grad_up, 'dp', scatter_dimension=0, tiled=True)  166 us
    reduce_scatter x1, waiting for transfers between devices, local(): lax.psum_scatter(grad_qkv_weight, 'dp', scatter_dimension=0, tiled=True)  98.8 us
    psum x1, waiting for transfers between devices, local(): lax.psum((owned[0], owned[1], owned[2], owned[3], owned[4]), 'head')  70 us
    all_gather x1, waiting for transfers between devices, local(): lax.all_gather(feedforward_master.astype(jnp.bfloat16), 'dp', axis=0, til...  65.3 us
    unnamed x9, waiting for transfers between devices  64.8 us
    all_gather x1, waiting for transfers between devices, local(): lax.all_gather(attention_master.astype(jnp.bfloat16), 'dp', axis=0, tiled...  47.5 us
    all_gather x1, blocking collectives, local(): lax.all_gather(vector_master.astype(jnp.bfloat16), 'dp', axis=1, tiled=True)  32.5 us
  transfers between devices with their start and end apart: 14, of which 12 were waited for; matrix products, arithmetic and copies ran while one was open for 12% of the time, Pallas kernels for 0%

commit v1 on v0

v1 whole, which is shorter than its diff:
```python
import functools

import jax
import jax.numpy as jnp
from jax import lax
from jax.experimental import pallas as pl
from jax.experimental.pallas import tpu as pltpu
from jax.sharding import PartitionSpec as P

HEADS = 12
HEAD_DIM = 64
ADAM_STEP = 3

norm_epsilon = 1e-06
beta_one = 0.5
beta_two = 0.5
adam_epsilon = 1e-08
learn_rate = 0.05
weight_decay = 0.05
teacher_keep = 0.8
clip_limit = 1.0
masked_score = -1e30

BF = jnp.bfloat16
F32 = jnp.float32


def dot_rows(left, right):
    return lax.dot_general(left, right, (((0,), (0,)), ((), ())), preferred_element_type=F32)


def dot_cols(left, right):
    return lax.dot_general(left, right, (((1,), (1,)), ((), ())), preferred_element_type=F32)


def dot(left, right):
    return jnp.dot(left, right, preferred_element_type=F32)


def normalize(values):
    center = jnp.mean(values, axis=-1, keepdims=True)
    deviate = values - center
    spread = jnp.mean(deviate * deviate, axis=-1, keepdims=True)
    inverse = lax.rsqrt(spread + norm_epsilon)
    return deviate * inverse, inverse


def norm_back(hat, inverse, gain, grad):
    scaled = grad * gain
    mean_one = jnp.mean(scaled, axis=-1, keepdims=True)
    mean_two = jnp.mean(scaled * hat, axis=-1, keepdims=True)
    return inverse * (scaled - mean_one - hat * mean_two)


def head_lanes(index, shape):
    lane = lax.broadcasted_iota(jnp.int32, shape, 1)
    return (lane >= index * HEAD_DIM) & (lane < (index + 1) * HEAD_DIM)


def attend_kernel(per, q_ref, k_ref, v_ref, seg_q_ref, seg_k_ref, out_ref):
    same = seg_q_ref[...] == seg_k_ref[...]
    queries = q_ref[...] * jnp.asarray(HEAD_DIM**-0.5, BF)
    keys = k_ref[...]
    values = v_ref[...]
    result = jnp.zeros(out_ref.shape, F32)
    for head in range(per):
        lanes = head_lanes(head, queries.shape)
        score = dot_cols(jnp.where(lanes, queries, jnp.zeros_like(queries)), keys)
        score = jnp.where(same, score, masked_score)
        largest = jnp.max(score, axis=1, keepdims=True)
        power = jnp.exp(score - largest)
        total = jnp.sum(power, axis=1, keepdims=True)
        chance = (power * (1.0 / total)).astype(BF)
        result = jnp.where(lanes, dot(chance, values), result)
    out_ref[...] = result.astype(BF)


def attend(qkv, segments, per):
    length = qkv.shape[0]
    cols = per * HEAD_DIM
    block = 256
    queries, keys, values = qkv[:, :cols], qkv[:, cols : 2 * cols], qkv[:, 2 * cols :]
    return pl.pallas_call(
        functools.partial(attend_kernel, per),
        out_shape=jax.ShapeDtypeStruct((length, cols), BF),
        grid=(length // block,),
        in_specs=[
            pl.BlockSpec((block, cols), lambda i: (i, 0)),
            pl.BlockSpec((length, cols), lambda i: (0, 0)),
            pl.BlockSpec((length, cols), lambda i: (0, 0)),
            pl.BlockSpec((block, 1), lambda i: (i, 0)),
            pl.BlockSpec((1, length), lambda i: (0, 0)),
        ],
        out_specs=pl.BlockSpec((block, cols), lambda i: (i, 0)),
        compiler_params=pltpu.CompilerParams(vmem_limit_bytes=48 * 2**20),
        name="attend",
    )(queries, keys, values, segments.reshape(length, 1), segments)


def attend_back_kernel(
    per, q_ref, k_ref, v_ref, do_ref, seg_q_ref, seg_k_ref, dq_ref, dk_ref, dv_ref, k_acc, v_acc
):
    step = pl.program_id(0)

    @pl.when(step == 0)
    def _():
        k_acc[...] = jnp.zeros_like(k_acc)
        v_acc[...] = jnp.zeros_like(v_acc)

    same = seg_k_ref[...] == seg_q_ref[...]
    queries = q_ref[...] * jnp.asarray(HEAD_DIM**-0.5, BF)
    grads = do_ref[...]
    keys = k_ref[...]
    values = v_ref[...]
    grad_query = jnp.zeros(dq_ref.shape, F32)
    for head in range(per):
        lanes = head_lanes(head, queries.shape)
        query = jnp.where(lanes, queries, jnp.zeros_like(queries))
        grad = jnp.where(lanes, grads, jnp.zeros_like(grads))
        score = jnp.where(same, dot_cols(keys, query), masked_score)
        largest = jnp.max(score, axis=0, keepdims=True)
        power = jnp.exp(score - largest)
        total = jnp.sum(power, axis=0, keepdims=True)
        chance = power * (1.0 / total)
        grad_chance = dot_cols(values, grad)
        inner = jnp.sum(chance * grad_chance, axis=0, keepdims=True)
        grad_score = (chance * (grad_chance - inner)).astype(BF)
        k_acc[...] += dot(grad_score, query)
        v_acc[...] += dot(chance.astype(BF), grad)
        grad_query = jnp.where(lanes, dot_rows(grad_score, keys), grad_query)
    dq_ref[...] = (grad_query * HEAD_DIM**-0.5).astype(BF)

    @pl.when(step == pl.num_programs(0) - 1)
    def _():
        dk_ref[...] = k_acc[...].astype(BF)
        dv_ref[...] = v_acc[...].astype(BF)


def attend_back(qkv, grad_out, segments, per):
    length = qkv.shape[0]
    cols = per * HEAD_DIM
    block = 256
    queries, keys, values = qkv[:, :cols], qkv[:, cols : 2 * cols], qkv[:, 2 * cols :]
    whole = pl.BlockSpec((length, cols), lambda i: (0, 0))
    part = pl.BlockSpec((block, cols), lambda i: (i, 0))
    shape = jax.ShapeDtypeStruct((length, cols), BF)
    return pl.pallas_call(
        functools.partial(attend_back_kernel, per),
        out_shape=(shape, shape, shape),
        grid=(length // block,),
        in_specs=[
            part,
            whole,
            whole,
            part,
            pl.BlockSpec((1, block), lambda i: (0, i)),
            pl.BlockSpec((length, 1), lambda i: (0, 0)),
        ],
        out_specs=(part, whole, whole),
        scratch_shapes=[pltpu.VMEM((length, cols), F32), pltpu.VMEM((length, cols), F32)],
        compiler_params=pltpu.CompilerParams(vmem_limit_bytes=48 * 2**20),
        name="attend_back",
    )(queries, keys, values, grad_out, segments, segments.reshape(length, 1))


def adam_update(master, moment, second, teacher, gradient, factor, decay_rate):
    clipped = gradient * factor
    moment_new = beta_one * moment + (1.0 - beta_one) * clipped
    second_new = beta_two * second + (1.0 - beta_two) * clipped * clipped
    scale_one = 1.0 - beta_one**ADAM_STEP
    scale_two = 1.0 - beta_two**ADAM_STEP
    update = moment_new / scale_one / (jnp.sqrt(second_new / scale_two) + adam_epsilon)
    master_new = master * (1.0 - learn_rate * decay_rate) - learn_rate * update
    teacher_new = teacher_keep * teacher + (1.0 - teacher_keep) * master_new
    return (master_new, moment_new, second_new, teacher_new)


PAIR_ROW = [[0, 2], [1, 3]]
PAIR_CORE = [[0, 1], [2, 3]]


def gather_head(part):
    rows = lax.all_gather(part, "head", axis=0, axis_index_groups=PAIR_ROW)
    both = lax.all_gather(rows, "head", axis=0, axis_index_groups=PAIR_CORE)
    return [both[0, 0], both[1, 0], both[0, 1], both[1, 1]]


def swap(part, bit):
    return lax.ppermute(part, "head", [(i, i ^ bit) for i in range(4)])


def scatter_head(partial, member):
    rows, width = partial.shape
    row, core = member // 2, member % 2
    blocks = partial.reshape(2, 2, rows // 4, width)
    keep = lax.dynamic_index_in_dim(blocks, core, 1, keepdims=False)
    send = lax.dynamic_index_in_dim(blocks, 1 - core, 1, keepdims=False).astype(BF)
    half = keep + swap(send, 1).astype(F32)
    keep = lax.dynamic_index_in_dim(half, row, 0, keepdims=False)
    send = lax.dynamic_index_in_dim(half, 1 - row, 0, keepdims=False).astype(BF)
    return keep + swap(send, 2).astype(F32)


def local(
    tokens,
    cotangent,
    segments,
    attention_master,
    feedforward_master,
    vector_master,
    attention_moment,
    feedforward_moment,
    vector_moment,
    attention_second,
    feedforward_second,
    vector_second,
    attention_teacher,
    feedforward_teacher,
    vector_teacher,
):
    width = tokens.shape[1]
    rows = tokens.shape[0]
    owners = lax.axis_size("dp")
    groups = lax.axis_size("head")
    member = lax.axis_index("head")
    hidden = feedforward_master.shape[1] // 2
    per = HEADS // groups
    cols = per * HEAD_DIM
    part = hidden // groups
    owned = attention_master.shape[0]

    def own_cols(array, start, size):
        return lax.dynamic_slice_in_dim(array, start + member * size, size, axis=1)

    low_qkv = jnp.concatenate(
        [own_cols(attention_master, i * width, cols) for i in range(3)], axis=1
    ).astype(BF)
    w_qkv = lax.all_gather(low_qkv, "dp", axis=0, tiled=True)
    vector_low = lax.all_gather(vector_master.astype(BF), "dp", axis=1, tiled=True)
    low_rest = jnp.concatenate(
        [
            attention_master[:, 3 * width :],
            own_cols(feedforward_master, 0, part),
            own_cols(feedforward_master, hidden, part),
        ],
        axis=1,
    ).astype(BF)
    w_rest = lax.all_gather(low_rest, "dp", axis=0, tiled=True)
    w_out = w_rest[:, :width]
    w_up = w_rest[:, width : width + part]
    w_down = w_rest[:, width + part :]

    vector_full = vector_low.astype(F32)
    gain_one, shift_one = vector_full[0], vector_full[1]
    output_bias, gain_two, shift_two, down_bias = (vector_full[i] for i in (4, 5, 6, 7))
    query_bias = lax.dynamic_slice_in_dim(vector_full[2], member * cols, cols)
    value_bias = lax.dynamic_slice_in_dim(vector_full[3], member * cols, cols)
    up_bias = lax.dynamic_index_in_dim(vector_full[8:12], member, 0, keepdims=False)

    inputs = jnp.concatenate(gather_head(tokens), axis=0).astype(F32)
    grads = jnp.concatenate(gather_head(cotangent), axis=0)

    hat_one, inverse_one = normalize(inputs)
    normed = (hat_one * gain_one + shift_one).astype(BF)
    qkv_bias = jnp.concatenate([query_bias, jnp.zeros_like(query_bias), value_bias])
    qkv = (dot(normed, w_qkv) + qkv_bias).astype(BF)
    attended = attend(qkv, segments, per)
    mixed = jnp.concatenate(gather_head(attended), axis=1)
    resid = inputs + dot(mixed, w_out) + output_bias
    hat_two, inverse_two = normalize(resid)
    normed_two = (hat_two * gain_two + shift_two).astype(BF)
    pre_act = dot(normed_two, w_up) + up_bias
    phi = 0.5 * (1.0 + lax.erf(pre_act * 0.7071067811865476))
    activated = (pre_act * phi).astype(BF)
    slope = phi + pre_act * (jnp.exp(-0.5 * pre_act * pre_act) * 0.3989422804014327)
    grad_pre = (dot(grads, w_down) * slope).astype(BF)
    branch = scatter_head(dot_cols(activated, w_down), member)

    def own_rows(array):
        return lax.dynamic_slice_in_dim(array, member * rows, rows, axis=0)

    resid_own = own_rows(resid)
    block_output = (resid_own + branch + down_bias).astype(BF)

    grad_down = dot_rows(grads, activated)
    grad_up = dot_rows(normed_two, grad_pre)
    grad_up_bias = jnp.sum(grad_pre.astype(F32), axis=0)
    grad_normed_two = dot_cols(grad_pre, w_up)
    grad_gain_two = jnp.sum(grad_normed_two * hat_two, axis=0)
    grad_shift_two = jnp.sum(grad_normed_two, axis=0)
    grad_two = scatter_head(grad_normed_two, member)
    grad_resid = cotangent.astype(F32) + norm_back(
        own_rows(hat_two), own_rows(inverse_two), gain_two, grad_two
    )
    grad_branch = grad_resid.astype(BF)
    grad_down_bias = jnp.sum(cotangent.astype(F32), axis=0)
    grad_out_bias = jnp.sum(grad_branch.astype(F32), axis=0)
    branch_all = jnp.concatenate(gather_head(grad_branch), axis=0)
    grad_out = dot_rows(mixed, lax.dynamic_slice_in_dim(branch_all, member * cols, cols, axis=1))
    w_out_own = lax.dynamic_slice_in_dim(w_out, member * cols, cols, axis=0)
    grad_mixed = dot_cols(branch_all, w_out_own).astype(BF)
    grad_query, grad_key, grad_value = attend_back(qkv, grad_mixed, segments, per)
    grad_qkv = jnp.concatenate([grad_query, grad_key, grad_value], axis=1)
    grad_qkv_weight = dot_rows(normed, grad_qkv)
    grad_query_bias = jnp.sum(grad_query.astype(F32), axis=0)
    grad_value_bias = jnp.sum(grad_value.astype(F32), axis=0)
    grad_normed = dot_cols(grad_qkv, w_qkv)
    grad_gain_one = jnp.sum(grad_normed * hat_one, axis=0)
    grad_shift_one = jnp.sum(grad_normed, axis=0)
    grad_one = scatter_head(grad_normed, member)
    input_gradient = grad_resid + norm_back(
        own_rows(hat_one), own_rows(inverse_one), gain_one, grad_one
    )

    def place(piece):
        return lax.dynamic_update_slice_in_dim(jnp.zeros((width,), F32), piece, member * cols, 0)

    up_rows = lax.dynamic_update_slice_in_dim(
        jnp.zeros((groups, part), F32), grad_up_bias[None], member, 0
    )
    grad_vector = jnp.concatenate(
        [
            jnp.stack(
                [
                    grad_gain_one,
                    grad_shift_one,
                    place(grad_query_bias),
                    place(grad_value_bias),
                    grad_out_bias,
                    grad_gain_two,
                    grad_shift_two,
                    grad_down_bias,
                ]
            ),
            up_rows,
        ],
        axis=0,
    )

    sum_ff = lax.psum_scatter(
        jnp.concatenate([grad_up, grad_down], axis=1).astype(BF),
        "dp",
        scatter_dimension=0,
        tiled=True,
    )
    vector_high = grad_vector.astype(BF)
    vector_rest = (grad_vector - vector_high.astype(F32)).astype(BF)
    vector_pack = jnp.concatenate([vector_high, vector_rest], axis=0).T
    attention_pack = jnp.concatenate(
        [grad_qkv_weight.astype(BF), grad_out.astype(BF), vector_pack], axis=1
    )
    pieces = lax.all_to_all(
        attention_pack.reshape(owners, owned, -1), "dp", split_axis=0, concat_axis=0
    )
    sum_pack = jnp.sum(pieces.astype(F32), axis=0)
    sum_attention = sum_pack[:, : 4 * cols].astype(BF)
    sum_vector = sum_pack[:, 4 * cols : 4 * cols + 12] + sum_pack[:, 4 * cols + 12 :]

    vectors = gather_head(sum_vector)
    vector_grad = (vectors[0] + vectors[1] + vectors[2] + vectors[3]).T
    attention_parts = gather_head(sum_attention)
    attention_grad = jnp.concatenate(
        [item[:, i * cols : (i + 1) * cols] for i in range(4) for item in attention_parts], axis=1
    ).astype(F32)
    forward_parts = gather_head(sum_ff)
    forward_grad = jnp.concatenate(
        [item[:, i * part : (i + 1) * part] for i in range(2) for item in forward_parts], axis=1
    ).astype(F32)
    squares = (
        jnp.sum(attention_grad * attention_grad)
        + jnp.sum(forward_grad * forward_grad)
        + jnp.sum(vector_grad * vector_grad)
    )
    total = jnp.sum(
        lax.all_to_all(
            jnp.broadcast_to(squares, (owners, 8, 128)), "dp", split_axis=0, concat_axis=0
        )[:, 0, 0]
    )
    gradient_norm = jnp.sqrt(total)
    factor = jnp.minimum(1.0, clip_limit / (gradient_norm + 1e-06))
    attention_new = adam_update(
        attention_master,
        attention_moment,
        attention_second,
        attention_teacher,
        attention_grad,
        factor,
        weight_decay,
    )
    forward_new = adam_update(
        feedforward_master,
        feedforward_moment,
        feedforward_second,
        feedforward_teacher,
        forward_grad,
        factor,
        weight_decay,
    )
    vector_new = adam_update(
        vector_master, vector_moment, vector_second, vector_teacher, vector_grad, factor, 0.0
    )
    states = []
    for state in range(4):
        states += [attention_new[state], forward_new[state], vector_new[state]]
    return (
        block_output,
        input_gradient,
        gradient_norm,
        *states,
        attention_new[0].astype(BF),
        forward_new[0].astype(BF),
        vector_new[0].astype(BF),
    )


def solution(mesh):
    rows = P(("dp", "head"), None)
    shard = P("dp", None)
    vector = P(None, "dp")
    return jax.shard_map(
        local,
        mesh=mesh,
        in_specs=(rows, rows, shard) + (shard, shard, vector) * 4,
        out_specs=(rows, rows, P()) + (shard, shard, vector) * 5,
        check_vma=False,
    )
```

time: 1010 us -> 475 us (0.47)
  waiting for transfers between devices: 705 us -> 122 us
  blocking collectives: 80.1 us -> 137 us
  matrix products: 71 us -> 32 us
  Pallas kernels: 0 us -> 24.6 us
  local copies, waits for them, and re-layouts: 56.3 us -> 78.5 us
    reduce_scatter x4 -> x1, waiting for transfers between devices: 432 us -> 0.02 us  [local(): lax.psum_scatter(jnp.concatenate([grad_up, grad_down], axis=1).astype(BF)...]
    all_gather x1 -> x11, blocking collectives: 32.5 us -> 137 us  [the longest x7 67.6 us: gather_head(): rows = lax.all_gather(part, 'head', axis=0, axis_index_groups=PAIR_ROW)]
    psum x1 -> x0, waiting for transfers between devices: 70 us -> none  [local(): lax.psum((owned[0], owned[1], owned[2], owned[3], owned[4]), 'head')]
    unnamed x9 -> x7, waiting for transfers between devices: 64.8 us -> 0.12 us
    all_gather x2 -> x6, waiting for transfers between devices: 113 us -> 72.3 us  [the longest x1 66.5 us: local(): w_rest = lax.all_gather(low_rest, 'dp', axis=0, tiled=True)]
    dot_general x33 -> x12, matrix products: 71 us -> 32 us  [the longest x4 12.2 us: dot(): return jnp.dot(left, right, preferred_element_type=F32)]
    psum x2 -> x0, blocking collectives: 27.8 us -> none  [the longest x1 22 us: local(): total = lax.psum(squares, 'dp')]
    pallas_call x0 -> x2, Pallas kernels: none -> 24.6 us  [the longest x1 17.1 us: attend_back(): pl.pallas_call(functools.partial(attend_back_kernel, per), out_shape=(sha...]
  transfers between devices with their start and end apart: 14 -> 15, of which waited for: 12 -> 6; matrix products, arithmetic and copies ran while one was open for 12% -> 22% of each run, Pallas kernels for 0% -> 5%
where the time goes in v1:
time: 475 us; the launch traced here: 469 us
  blocking collectives  137 us (29%)
  waiting for transfers between devices  122 us (26%)
  local copies, waits for them, and re-layouts  78.5 us (17%)
  other arithmetic  42.5 us (9%)
  matrix products  32 us (7%)
  Pallas kernels  24.6 us (5%)
  between operations  19.4 us (4%)
  starting transfers between devices  12.6 us (3%)
    all_gather x7, blocking collectives, gather_head(): rows = lax.all_gather(part, 'head', axis=0, axis_index_groups=PAIR_ROW)  67.6 us
    all_gather x1, waiting for transfers between devices, local(): w_rest = lax.all_gather(low_rest, 'dp', axis=0, tiled=True)  66.5 us
    all_gather x1, blocking collectives, local(): w_qkv = lax.all_gather(low_qkv, 'dp', axis=0, tiled=True)  34.1 us
    all_gather x1, blocking collectives, local(): lax.all_gather(vector_master.astype(BF), 'dp', axis=1, tiled=True)  31.2 us
    all_to_all x1, waiting for transfers between devices, local(): lax.all_to_all(attention_pack.reshape(owners, owned, -1), 'dp', split_axi...  29.5 us
    unnamed x167, local copies, waits for them, and re-layouts  25.5 us
    ppermute x6, waiting for transfers between devices, swap(): return lax.ppermute(part, 'head', [(i, i ^ bit) for i in range(4)])  17.3 us
    dynamic_slice x6, local copies, waits for them, and re-layouts, scatter_head(): keep = lax.dynamic_index_in_dim(blocks, core, 1, keepdims=False)  17.1 us
  transfers between devices with their start and end apart: 15, of which 6 were waited for; matrix products, arithmetic and copies ran while one was open for 22% of the time, Pallas kernels for 5%

profile of v1, /device:TPU:0, one launch (start us, length us, event | category | flops | bytes accessed | tf_op | source)
XLA Modules:
  0.0 468.5 jit_solution(18046561711134048156)
XLA Ops:
  7.3 14.8 %all-gather = bf16[512,768]{1,0:T(8,128)(2,1)} all-gather(bf16[256,768]{1,0:T(8,128)(2,1)} %param.15), channel_id=2, replica_groups={{0,2},{1,3},{4,6},{5,7},{8,10},{9,11},{12,14},{13,15},{16,18},{17,19},{..., dimensions={0}, use_global_device_ids=true | all-gather | bytes 1179648 | tf_op jit(solution)/shard_map/all_gather | solution.py:183
  22.1 11.3 %all-gather.4 = bf16[512,768]{1,0:T(8,128)(2,1)} all-gather(bf16[256,768]{1,0:T(8,128)(2,1)} %param.16), channel_id=6, replica_groups={{0,2},{1,3},{4,6},{5,7},{8,10},{9,11},{12,14},{13,15},{16,18},{17,19},{..., dimensions={0}, use_global_device_ids=true | all-gather | bytes 1179648 | tf_op jit(solution)/shard_map/all_gather | solution.py:183
  33.5 31.2 %all-gather.14 = bf16[8,96,12]{1,2,0:T(8,128)(2,1)S(1)} all-gather(bf16[1,96,12]{1,2,0:T(8,128)(2,1)S(1)} %convert_bitcast_fusion.3), channel_id=1, replica_groups=mesh['dp'=8,'head'=4] {'dp'}, dimensions={0}, use_global_device_ids=true | all-gather | bytes 20736 | tf_op jit(solution)/shard_map/all_gather | solution.py:239
  67.0 34.1 %all_gather.98 = bf16[768,576]{1,0:T(8,128)(2,1)} all-gather(bf16[96,576]{1,0:T(8,128)(2,1)S(1)} %pad_maximum_fusion.14), channel_id=1, replica_groups=mesh['dp'=8,'head'=4] {'dp'}, dimensions={0}, use_global_device_ids=true | all-gather | bytes 995328 | tf_op jit(solution)/shard_map/all_gather | solution.py:238
  101.2 1.7 copy.137
  104.6 1.7 add_convert_fusion.2
  106.6 7.6 %attend.1 = bf16[1024,192]{1,0:T(8,128)(2,1)S(1)} custom-call(bf16[1024,192]{1,0:T(8,128)(2,1)S(1)} %get-tuple-element.182.q_ref, bf16[1024,192]{1,0:T(8,128)(2,1)S(1)} %get-tuple-element.181.k_ref, bf16[1024,192]{1,0:T(8,128)(2,1)S(1)} %get-tuple-element.180.v_ref, s32[1024,1]{1,0:T(8,128)S(1)} %copy.140.seg_q_ref.seg_k_ref, s32[1,1024]{1,0:T(1,128)S(1)} %copy-done.2), custom_call_target="tpu_custom_call" | custom-call | tf_op jit(solution)/shard_map/attend/pallas_call | solution.py:83
  114.2 10.0 %all-gather.2 = bf16[2048,192]{1,0:T(8,128)(2,1)} all-gather(bf16[1024,192]{1,0:T(8,128)(2,1)S(1)} %attend.1), channel_id=4, replica_groups={{0,2},{1,3},{4,6},{5,7},{8,10},{9,11},{12,14},{13,15},{16,18},{17,19},{..., dimensions={0}, use_global_device_ids=true | all-gather | bytes 1179648 | tf_op jit(solution)/shard_map/all_gather | solution.py:183
  124.1 2.2 copy.141
  129.6 2.5 slice_bitcast_fusion.7
  132.1 5.7 %all-gather.27.cloned.1.call-done = bf16[4,1024,192]{1,2,0:T(8,128)(2,1)} async-done(((bf16[2,1024,192]{1,2,0:T(8,128)(2,1)}), bf16[4,1024,192]{1,2,0:T(8,128)(2,1)}) %all-gather.27.cloned.1.call-update) | async-done | bytes 1572880 | tf_op jit(solution)/shard_map/all_gather | solution.py:184
  137.9 2.5 slice_bitcast_fusion.11
  140.4 66.5 %all-gather.23.cloned.1.call-done = bf16[768,2304]{1,0:T(8,128)(2,1)} async-done(((bf16[96,2304]{1,0:T(8,128)(2,1)}), bf16[768,2304]{1,0:T(8,128)(2,1)}) %all-gather.23.cloned.1.call-update) | async-done | bytes 3538960 | tf_op jit(solution)/shard_map/all_gather | solution.py:248
  206.9 3.5 fusion.60
  212.1 2.6 copy-done.37
  214.7 3.2 multiply_convert_fusion
  217.9 3.8 convert_reduce_fusion.1
  221.8 1.4 fusion.62
  223.2 1.7 copy-done.11
  226.2 2.7 constant_dynamic-slice_fusion.3
  228.9 3.0 copy.145
  231.9 1.6 bitcast_add_fusion.1
  235.4 1.5 collective-permute-start.3
  238.2 9.0 %collective-permute-done.3 = bf16[256,768]{0,1:T(8,128)(2,1)S(1)} collective-permute-done((bf16[256,768]{0,1:T(8,128)(2,1)}, bf16[256,768]{0,1:T(8,128)(2,1)S(1)}, u32[]{:S(2)}, u32[]{:S(2)}) %collective-permute-start.3) | collective-permute-done | bytes 393248 | tf_op jit(solution)/shard_map/ppermute | solution.py:189
  247.2 1.7 fusion.46
  249.0 1.6 convert_reduce_fusion.6
  250.6 11.4 %all-gather.6 = bf16[512,768]{0,1:T(8,128)(2,1)S(1)} all-gather(bf16[256,768]{0,1:T(8,128)(2,1)S(1)} %get-tuple-element.159), channel_id=8, replica_groups={{0,2},{1,3},{4,6},{5,7},{8,10},{9,11},{12,14},{13,15},{16,18},{17,19},{..., dimensions={0}, use_global_device_ids=true | all-gather | bytes 1179648 | tf_op jit(solution)/shard_map/all_gather | solution.py:183
  263.4 3.5 convolution_convert_fusion
  266.9 1.9 convolution_convert_fusion.1
  268.8 1.6 pad_maximum_fusion
  270.4 4.3 copy.162
  274.7 3.2 fusion.15
  277.9 1.6 copy-done.33
  281.4 3.5 copy.153
  285.6 2.7 constant_dynamic-slice_fusion.5
  288.2 3.0 copy.142
  291.2 3.4 multiply_reduce_fusion
  298.8 1.5 collective-permute-start.1
  300.9 1.5 slice_bitcast_fusion.3
  305.1 17.1 %attend_back.1 = (bf16[1024,192]{1,0:T(8,128)(2,1)S(1)}, bf16[1024,192]{1,0:T(8,128)(2,1)S(1)}, bf16[1024,192]{1,0:T(8,128)(2,1)S(1)}) custom-call(bf16[1024,192]{1,0:T(8,128)(2,1)S(1)} %get-tuple-element.182.q_ref, bf16[1024,192]{1,0:T(8,128)(2,1)S(1)} %get-tuple-element.181.k_ref, bf16[1024,192]{1,0:T(8,128)(2,1)S(1)} %get-tuple-element.180.v_ref, ...), custom_call_target="tpu_custom_call" | custom-call | tf_op jit(solution)/shard_map/attend_back/pallas_call | solution.py:147
  322.2 3.2 fusion.61
  326.0 3.5 copy.152
  329.5 1.6 constant_dynamic-slice_fusion
  331.7 2.7 constant_dynamic-slice_fusion.1
  334.3 3.1 copy.150
  337.5 4.1 multiply_reduce_fusion.1
  343.2 3.3 convolution_convert_fusion.4
  348.6 2.7 convolution_convert_fusion.2
  351.2 8.3 %collective-permute-done.5 = bf16[256,768]{0,1:T(8,128)(2,1)S(1)} collective-permute-done((bf16[256,768]{0,1:T(8,128)(2,1)S(1)}, bf16[256,768]{0,1:T(8,128)(2,1)S(1)}, u32[]{:S(2)}, u32[]{:S(2)}) %collective-permute-start.5) | collective-permute-done | bytes 393248 | tf_op jit(solution)/shard_map/ppermute | solution.py:189
  361.7 9.8 %all-gather.10 = bf16[192,1536]{1,0:T(8,128)(2,1)} all-gather(bf16[96,1536]{1,0:T(8,128)(2,1)} %reduce-scatter.4.cloned.1.call-done), channel_id=12, replica_groups={{0,2},{1,3},{4,6},{5,7},{8,10},{9,11},{12,14},{13,15},{16,18},{17,19},{..., dimensions={0}, use_global_device_ids=true | all-gather | bytes 884736 | tf_op jit(solution)/shard_map/all_gather | solution.py:183
  371.7 3.3 convert_reduce_fusion.5
  376.3 1.6 copy.154
  377.8 3.6 all-to-all-start
  384.1 29.5 %all-to-all-done = bf16[8,96,792]{2,1,0:T(8,128)(2,1)S(1)} async-done(((bf16[8,96,792]{2,1,0:T(8,128)(2,1)}), bf16[8,96,792]{2,1,0:T(8,128)(2,1)S(1)}, u32[]{:S(2)}, u32[]{:S(2)}) %all-to-all-start) | async-done | bytes 1216544 | tf_op jit(solution)/shard_map/all_to_all | solution.py:352
  413.8 6.0 %all-gather.8 = bf16[192,768]{1,0:T(8,128)(2,1)S(1)} all-gather(bf16[96,768]{1,0:T(8,128)(2,1)S(1)} %slice.428), channel_id=10, replica_groups={{0,2},{1,3},{4,6},{5,7},{8,10},{9,11},{12,14},{13,15},{16,18},{17,19},{..., dimensions={0}, use_global_device_ids=true | all-gather | bytes 442368 | tf_op jit(solution)/shard_map/all_gather | solution.py:183
  419.8 2.2 all-gather.9
  425.3 4.4 all-gather.15
  429.6 1.8 all-gather.13
  433.3 4.5 all-to-all-start.1
  437.9 1.7 fusion.25
  441.7 2.9 all-to-all-done.1
  447.1 4.5 fusion.51
  454.1 4.1 fusion.49
  458.2 2.1 multiply_add_fusion.1
  (273 shorter events, 45.9 us)
Async XLA Ops:
  7.2 26.3 %copy-start.48 = (f32[12,96]{1,0:T(8,128)S(1)}, f32[12,96]{1,0:T(8,128)}, u32[]{:S(2)}) copy-start(f32[12,96]{1,0:T(8,128)} %param.20) | copy-start | bytes 13828
  7.2 58.2 %copy-start.2 = (s32[1,1024]{1,0:T(1,128)S(1)}, s32[1,1024]{1,0:T(1,128)}, u32[]{:S(2)}) copy-start(s32[1,1024]{1,0:T(1,128)} %seg_q_ref.1) | copy-start | bytes 12292
  7.2 94.0 %all-gather.25.cloned.1.call-start = ((), (), s32[]{:S(2)}) async-start(), calls=%async_computation.4 | async-start | bytes 2359296 | tf_op jit(solution)/shard_map/all_gather | solution.py:184
  22.0 107.6 %all-gather.29.cloned.1.call-start = ((), (), s32[]{:S(2)}) async-start(), calls=%async_computation.6 | async-start | bytes 2359296 | tf_op jit(solution)/shard_map/all_gather | solution.py:184
  33.4 104.5 %all-gather.27.cloned.1.call-start = ((), (), s32[]{:S(2)}) async-start(), calls=%async_computation.5 | async-start | bytes 2359296 | tf_op jit(solution)/shard_map/all_gather | solution.py:184
  65.4 38.4 %copy-start.71 = (f32[768]{0:T(1024)}, f32[768]{0:T(1024)S(1)}, u32[]{:S(2)}) copy-start(f32[768]{0:T(1024)S(1)} %get-tuple-element.215) | copy-start | bytes 9220
  103.0 3.3 copy-start.18
  103.0 103.9 %copy-start.14 = (bf16[256,768]{0,1:T(8,128)(2,1)}, bf16[256,768]{0,1:T(8,128)(2,1)S(1)}, u32[]{:S(2)}) copy-start(bf16[256,768]{0,1:T(8,128)(2,1)S(1)} %get-tuple-element.177) | copy-start | bytes 1179652
  103.0 103.9 %copy-start.16 = (bf16[256,768]{0,1:T(8,128)(2,1)}, bf16[256,768]{0,1:T(8,128)(2,1)S(1)}, u32[]{:S(2)}) copy-start(bf16[256,768]{0,1:T(8,128)(2,1)S(1)} %get-tuple-element.178) | copy-start | bytes 1179652
  103.8 177.0 %copy-start.50 = (f32[1024]{0:T(1024)}, f32[1024]{0:T(1024)S(1)}, u32[]{:S(2)}) copy-start(f32[1024]{0:T(1024)S(1)} %add_rsqrt_fusion.1) | copy-start | bytes 12292
  126.3 80.5 %all-gather.23.cloned.1.call-start = ((), (), s32[]{:S(2)}) async-start(), calls=%async_computation.3 | async-start | bytes 3981312 | tf_op jit(solution)/shard_map/all_gather | solution.py:248
  129.3 171.6 %all-gather.31.cloned.1.call-start = ((), (), s32[]{:S(2)}) async-start(), calls=%async_computation.7 | async-start | bytes 2359296 | tf_op jit(solution)/shard_map/all_gather | solution.py:184
  210.8 3.8 copy-start.37
  212.1 5.8 %copy-start.9 = (f32[1024,768]{0,1:T(8,128)}, f32[1024,768]{0,1:T(8,128)S(1)}, u32[]{:S(2)}) copy-start(f32[1024,768]{0,1:T(8,128)S(1)} %subtract_multiply_fusion) | copy-start | bytes 9437188
  226.2 5.7 %collective-permute-start.2 = (bf16[2,256,768]{1,2,0:T(8,128)(2,1)}, bf16[2,256,768]{1,2,0:T(8,128)(2,1)S(1)}, u32[]{:S(2)}, u32[]{:S(2)}) collective-permute-start(bf16[2,256,768]{1,2,0:T(8,128)(2,1)} %bitcast.167), channel_id=1, source_target_pairs={{0,1},{1,0},{2,3},{3,2},{4,5},{5,4},{6,7},{7,6},{8,9},{9,8},{10,11... | collective-permute-start | bytes 2359304 | tf_op jit(solution)/shard_map/ppermute | solution.py:189
  235.4 11.7 %collective-permute-start.3 = (bf16[256,768]{0,1:T(8,128)(2,1)}, bf16[256,768]{0,1:T(8,128)(2,1)S(1)}, u32[]{:S(2)}, u32[]{:S(2)}) collective-permute-start(bf16[256,768]{0,1:T(8,128)(2,1)} %fusion.29), channel_id=1, source_target_pairs={{0,2},{1,3},{2,0},{3,1},{4,6},{5,7},{6,4},{7,5},{8,10},{9,11},{10,... | collective-permute-start | bytes 1179656 | tf_op jit(solution)/shard_map/ppermute | solution.py:189
  238.1 12.4 %copy-start.24 = (bf16[256,768]{0,1:T(8,128)(2,1)}, bf16[256,768]{0,1:T(8,128)(2,1)S(1)}, u32[]{:S(2)}) copy-start(bf16[256,768]{0,1:T(8,128)(2,1)S(1)} %copy.144) | copy-start | bytes 1179652
  238.1 10.8 %copy-start.7 = (f32[2,256,768]{1,2,0:T(8,128)S(1)}, f32[2,256,768]{1,2,0:T(8,128)}, u32[]{:S(2)}) copy-start(f32[2,256,768]{1,2,0:T(8,128)} %copy-done.6) | copy-start | bytes 4718596
  238.2 12.3 %copy-start.62 = (f32[256]{0:T(256)}, f32[256]{0:T(256)S(1)}, u32[]{:S(2)}) copy-start(f32[256]{0:T(256)S(1)} %dynamic-slice.8) | copy-start | bytes 3076
  247.2 3.4 copy-start.26
  248.9 14.2 %copy-start.64 = (f32[256]{0:T(256)}, f32[256]{0:T(256)S(1)}, u32[]{:S(2)}) copy-start(f32[256]{0:T(256)S(1)} %broadcast_multiply_fusion.5) | copy-start | bytes 3076
  248.9 14.2 %copy-start.66 = (f32[256]{0:T(256)}, f32[256]{0:T(256)S(1)}, u32[]{:S(2)}) copy-start(f32[256]{0:T(256)S(1)} %broadcast_multiply_fusion.4) | copy-start | bytes 3076
  263.2 98.5 %reduce-scatter.4.cloned.1.call-start = ((), (), s32[]{:S(2)}) async-start(), calls=%async_computation.9 | async-start | bytes 2654208 | tf_op jit(solution)/shard_map/reduce_scatter | solution.py:340
  263.4 3.5 copy-start.10
  263.4 3.5 copy-start.75
  274.7 106.7 %all-gather.33.cloned.1.call-start = ((), (), s32[]{:S(2)}) async-start(), calls=%async_computation.8 | async-start | bytes 1769472 | tf_op jit(solution)/shard_map/all_gather | solution.py:184
  280.8 14.5 %collective-permute-start = (bf16[2,256,768]{1,2,0:T(8,128)(2,1)}, bf16[2,256,768]{1,2,0:T(8,128)(2,1)S(1)}, u32[]{:S(2)}, u32[]{:S(2)}) collective-permute-start(bf16[2,256,768]{1,2,0:T(8,128)(2,1)} %bitcast.169), channel_id=1, source_target_pairs={{0,1},{1,0},{2,3},{3,2},{4,5},{5,4},{6,7},{7,6},{8,9},{9,8},{10,11... | collective-permute-start | bytes 2359304 | tf_op jit(solution)/shard_map/ppermute | solution.py:189
  298.8 139.0 %collective-permute-start.1 = (bf16[256,768]{0,1:T(8,128)(2,1)}, bf16[256,768]{0,1:T(8,128)(2,1)}, u32[]{:S(2)}, u32[]{:S(2)}) collective-permute-start(bf16[256,768]{0,1:T(8,128)(2,1)} %fusion.28), channel_id=1, source_target_pairs={{0,2},{1,3},{2,0},{3,1},{4,6},{5,7},{6,4},{7,5},{8,10},{9,11},{10,... | collective-permute-start | bytes 1179656 | tf_op jit(solution)/shard_map/ppermute | solution.py:189
  305.1 17.1 %copy-start.39 = (bf16[768,576]{1,0:T(8,128)(2,1)S(1)}, bf16[768,576]{1,0:T(8,128)(2,1)}, u32[]{:S(2)}) copy-start(bf16[768,576]{1,0:T(8,128)(2,1)} %all_gather.98) | copy-start | bytes 2654212
  331.4 15.1 %collective-permute-start.4 = (bf16[2,256,768]{1,2,0:T(8,128)(2,1)S(1)}, bf16[2,256,768]{1,2,0:T(8,128)(2,1)}, u32[]{:S(2)}, u32[]{:S(2)}) collective-permute-start(bf16[2,256,768]{1,2,0:T(8,128)(2,1)S(1)} %bitcast.168), channel_id=1, source_target_pairs={{0,1},{1,0},{2,3},{3,2},{4,5},{5,4},{6,7},{7,6},{8,9},{9,8},{10,11... | collective-permute-start | bytes 2359304 | tf_op jit(solution)/shard_map/ppermute | solution.py:189
  337.5 5.0 %copy-start.1 = (bf16[1024,192]{1,0:T(8,128)(2,1)S(1)}, bf16[1024,192]{1,0:T(8,128)(2,1)}, u32[]{:S(2)}) copy-start(bf16[1024,192]{1,0:T(8,128)(2,1)} %copy-done) | copy-start | bytes 1179652
  343.2 3.3 copy-start.20
  347.9 11.7 %copy-start.13 = (f32[2,256,768]{1,2,0:T(8,128)}, f32[2,256,768]{1,2,0:T(8,128)S(1)}, u32[]{:S(2)}) copy-start(f32[2,256,768]{1,2,0:T(8,128)S(1)} %bitcast_add_fusion) | copy-start | bytes 4718596
  347.9 11.6 %collective-permute-start.5 = (bf16[256,768]{0,1:T(8,128)(2,1)S(1)}, bf16[256,768]{0,1:T(8,128)(2,1)S(1)}, u32[]{:S(2)}, u32[]{:S(2)}) collective-permute-start(bf16[256,768]{0,1:T(8,128)(2,1)S(1)} %fusion.30), channel_id=1, source_target_pairs={{0,2},{1,3},{2,0},{3,1},{4,6},{5,7},{6,4},{7,5},{8,10},{9,11},{10,... | collective-permute-start | bytes 1179656 | tf_op jit(solution)/shard_map/ppermute | solution.py:189
  351.2 20.4 %copy-start.8 = (f32[2,256,768]{1,2,0:T(8,128)S(1)}, f32[2,256,768]{1,2,0:T(8,128)}, u32[]{:S(2)}) copy-start(f32[2,256,768]{1,2,0:T(8,128)} %copy-done.6) | copy-start | bytes 4718596
  351.2 20.4 %copy-start.25 = (bf16[256,768]{0,1:T(8,128)(2,1)S(1)}, bf16[256,768]{0,1:T(8,128)(2,1)}, u32[]{:S(2)}) copy-start(bf16[256,768]{0,1:T(8,128)(2,1)} %copy-done.24) | copy-start | bytes 1179652
  351.2 20.4 %copy-start.27 = (bf16[256,768]{0,1:T(8,128)(2,1)S(1)}, bf16[256,768]{0,1:T(8,128)(2,1)}, u32[]{:S(2)}) copy-start(bf16[256,768]{0,1:T(8,128)(2,1)} %copy-done.26) | copy-start | bytes 1179652
  351.2 20.4 %copy-start.63 = (f32[256]{0:T(256)S(1)}, f32[256]{0:T(256)}, u32[]{:S(2)}) copy-start(f32[256]{0:T(256)} %copy-done.62) | copy-start | bytes 3076
  351.2 20.4 %copy-start.65 = (f32[256]{0:T(256)S(1)}, f32[256]{0:T(256)}, u32[]{:S(2)}) copy-start(f32[256]{0:T(256)} %copy-done.64) | copy-start | bytes 3076
  351.2 20.4 %copy-start.67 = (f32[256]{0:T(256)S(1)}, f32[256]{0:T(256)}, u32[]{:S(2)}) copy-start(f32[256]{0:T(256)} %copy-done.66) | copy-start | bytes 3076
  351.2 20.4 %copy-start.73 = (f32[256]{0:T(256)S(1)}, f32[256]{0:T(256)}, u32[]{:S(2)}) copy-start(f32[256]{0:T(256)} %dynamic-slice.9) | copy-start | bytes 3076
  371.6 3.4 copy-start.46
  371.6 3.4 copy-start.53
  371.7 3.4 copy-start.54
  371.7 3.4 copy-start.55
  371.7 3.4 copy-start.56
  371.7 3.4 copy-start.57
  371.7 3.4 copy-start.59
  371.7 3.4 copy-start.61
  371.7 3.5 copy-start.40
  377.8 35.7 %all-to-all-start = ((bf16[8,96,792]{2,1,0:T(8,128)(2,1)}), bf16[8,96,792]{2,1,0:T(8,128)(2,1)S(1)}, u32[]{:S(2)}, u32[]{:S(2)}) async-start(bf16[8,96,792]{2,1,0:T(8,128)(2,1)} %bitcast.48), calls=%async_computation | async-start | bytes 2752512 | tf_op jit(solution)/shard_map/all_to_all | solution.py:352
  422.0 15.9 %copy-start.52 = (f32[768]{0:T(1024)S(1)}, f32[768]{0:T(1024)}, u32[]{:S(2)}) copy-start(f32[768]{0:T(1024)} %get-tuple-element.219) | copy-start | bytes 9220
  422.6 17.9 %copy-start.28 = (f32[256,768]{0,1:T(8,128)S(1)}, f32[256,768]{0,1:T(8,128)}, u32[]{:S(2)}) copy-start(f32[256,768]{0,1:T(8,128)} %get-tuple-element.195) | copy-start | bytes 2359300
  433.3 11.2 %all-to-all-start.1 = ((f32[8,8,128]{2,1,0:T(8,128)}), f32[8,8,128]{2,1,0:T(8,128)S(1)}, u32[]{:S(2)}, u32[]{:S(2)}) async-start(f32[8,8,128]{2,1,0:T(8,128)} %broadcast_in_dim.11), calls=%async_computation.1 | async-start | bytes 65536 | tf_op jit(solution)/shard_map/all_to_all | solution.py:375
  437.9 8.0 %copy-start.49 = (f32[12,96]{1,0:T(8,128)S(1)}, f32[12,96]{1,0:T(8,128)}, u32[]{:S(2)}) copy-start(f32[12,96]{1,0:T(8,128)} %param.20) | copy-start | bytes 13828
  437.9 8.0 %copy-start.68 = (f32[12,96]{1,0:T(8,128)S(1)}, f32[12,96]{1,0:T(8,128)}, u32[]{:S(2)}) copy-start(f32[12,96]{1,0:T(8,128)} %param.23) | copy-start | bytes 13828
  437.9 8.0 %copy-start.69 = (f32[12,96]{1,0:T(8,128)S(1)}, f32[12,96]{1,0:T(8,128)}, u32[]{:S(2)}) copy-start(f32[12,96]{1,0:T(8,128)} %param.26) | copy-start | bytes 13828
  437.9 8.6 %copy-start.70 = (f32[12,96]{1,0:T(8,128)S(1)}, f32[12,96]{1,0:T(8,128)}, u32[]{:S(2)}) copy-start(f32[12,96]{1,0:T(8,128)} %param.29) | copy-start | bytes 13828
  446.5 5.1 %copy-start.47 = (f32[12,96]{1,0:T(8,128)}, f32[12,96]{1,0:T(8,128)S(1)}, u32[]{:S(2)}) copy-start(f32[12,96]{1,0:T(8,128)S(1)} %get-tuple-element.143) | copy-start | bytes 13828
  447.1 4.5 copy-start.36
  447.1 5.7 %copy-start.30 = (f32[96,6144]{1,0:T(8,128)S(1)}, f32[96,6144]{1,0:T(8,128)}, u32[]{:S(2)}) copy-start(f32[96,6144]{1,0:T(8,128)} %param.22) | copy-start | bytes 7077892
  447.1 5.7 %copy-start.31 = (f32[96,6144]{1,0:T(8,128)S(1)}, f32[96,6144]{1,0:T(8,128)}, u32[]{:S(2)}) copy-start(f32[96,6144]{1,0:T(8,128)} %param.25) | copy-start | bytes 7077892
  451.6 6.6 %copy-start.23 = (f32[96,3072]{1,0:T(8,128)}, f32[96,3072]{1,0:T(8,128)S(1)}, u32[]{:S(2)}) copy-start(f32[96,3072]{1,0:T(8,128)S(1)} %get-tuple-element.151) | copy-start | bytes 3538948
  454.1 4.1 copy-start.32
  (28 other events, 61.8 us)
Sparse Core Ops, SparseCore 0:
  22.2 10.0 all-gather.24
  33.8 11.1 all-gather.28
  126.5 11.3 all-gather.26
  140.5 66.3 all-gather.22
  263.3 8.2 all-gather.30
  275.5 70.0 reduce-scatter.3
  371.7 8.2 all-gather.32

commit v2 on v1

v2 whole, which is shorter than its diff:
```python
import functools

import jax
import jax.numpy as jnp
import numpy as np
from jax import lax
from jax.experimental import pallas as pl
from jax.experimental.pallas import tpu as pltpu
from jax.sharding import PartitionSpec as P

HEADS = 12
HEAD_DIM = 64
ADAM_STEP = 3

norm_epsilon = 1e-06
beta_one = 0.5
beta_two = 0.5
adam_epsilon = 1e-08
learn_rate = 0.05
weight_decay = 0.05
teacher_keep = 0.8
clip_limit = 1.0
masked_score = -1e30

BF = jnp.bfloat16
F32 = jnp.float32


def dot_rows(left, right):
    return lax.dot_general(left, right, (((0,), (0,)), ((), ())), preferred_element_type=F32)


def dot_cols(left, right):
    return lax.dot_general(left, right, (((1,), (1,)), ((), ())), preferred_element_type=F32)


def dot(left, right):
    return jnp.dot(left, right, preferred_element_type=F32)


def normalize(values):
    center = jnp.mean(values, axis=-1, keepdims=True)
    deviate = values - center
    spread = jnp.mean(deviate * deviate, axis=-1, keepdims=True)
    inverse = lax.rsqrt(spread + norm_epsilon)
    return deviate * inverse, inverse


def norm_back(hat, inverse, gain, grad):
    scaled = grad * gain
    mean_one = jnp.mean(scaled, axis=-1, keepdims=True)
    mean_two = jnp.mean(scaled * hat, axis=-1, keepdims=True)
    return inverse * (scaled - mean_one - hat * mean_two)


def head_lanes(index, shape):
    lane = lax.broadcasted_iota(jnp.int32, shape, 1)
    return (lane >= index * HEAD_DIM) & (lane < (index + 1) * HEAD_DIM)


def unit_rows(rows, columns):
    row = lax.broadcasted_iota(jnp.int32, (rows, columns), 0)
    column = lax.broadcasted_iota(jnp.int32, (rows, columns), 1)
    return jnp.where(row == column, 1.0, 0.0).astype(BF)


def smem():
    return pl.BlockSpec(memory_space=pltpu.SMEM)


def vmem():
    return pl.BlockSpec(memory_space=pltpu.VMEM)


def whole(*shape):
    return pl.BlockSpec(shape, lambda *index: (0,) * len(shape))


def shaped(shape, kind):
    return jax.ShapeDtypeStruct(shape, kind)


def params(mebibytes):
    return pltpu.CompilerParams(vmem_limit_bytes=mebibytes * 2**20)


COST_SCALE = 1.0


def cost(microseconds):
    return pl.CostEstimate(
        flops=0, transcendentals=0, bytes_accessed=int(microseconds * COST_SCALE * 3.6e6)
    )


def pin(array):
    return pltpu.with_memory_space_constraint(array, pltpu.HBM)


def far_space():
    return pl.BlockSpec(memory_space=pltpu.HBM)


def run(
    kernel, name, outputs, inputs, microseconds, scratch=(), mebibytes=16, lazy=(), save=(), far=()
):
    single = not isinstance(outputs, tuple)
    outputs = [outputs] if single else list(outputs)
    lazy, save, far = list(lazy), list(save), list(far)
    count, produced, own = len(inputs), len(outputs), len(scratch)
    buffers = [pltpu.VMEM(inputs[i].shape, inputs[i].dtype) for i in lazy]
    buffers += [pltpu.VMEM(outputs[i].shape, outputs[i].dtype) for i in far]
    moves = len(lazy) + len(save) + len(far)
    if moves:
        buffers.append(pltpu.SemaphoreType.DMA((moves,)))

    def body(*refs):
        items = list(refs[: count + produced])
        saved = refs[count + produced : count + produced + len(save)]
        rest = refs[count + produced + len(save) :]
        inner, extra = rest[:own], rest[own:]
        copies, number = [], 0
        for j, i in enumerate(lazy):
            copies.append(pltpu.make_async_copy(refs[i], extra[j], extra[-1].at[number]))
            items[i] = extra[j]
            number += 1
        stores = []
        for j, i in enumerate(save):
            stores.append(pltpu.make_async_copy(refs[i], saved[j], extra[-1].at[number]))
            number += 1
        last = []
        for j, i in enumerate(far):
            buffer = extra[len(lazy) + j]
            last.append(pltpu.make_async_copy(buffer, refs[count + i], extra[-1].at[number]))
            items[count + i] = buffer
            number += 1
        for copy in copies + stores:
            copy.start()
        for copy in copies:
            copy.wait()
        kernel(*items, *inner)
        for copy in last:
            copy.start()
        for copy in stores + last:
            copy.wait()

    shapes = [pltpu.HBM(item.shape, item.dtype) if i in far else item for i, item in enumerate(outputs)]
    results = pl.pallas_call(
        body,
        out_shape=shapes + [pltpu.HBM(inputs[i].shape, inputs[i].dtype) for i in save],
        in_specs=[smem()] + [far_space() if i in lazy else vmem() for i in range(1, count)],
        out_specs=[far_space() if i in far else vmem() for i in range(produced)]
        + [far_space()] * len(save),
        scratch_shapes=list(scratch) + buffers,
        compiler_params=params(mebibytes),
        cost_estimate=cost(microseconds),
        name=name,
    )(*[pin(item) if i in lazy else item for i, item in enumerate(inputs)])
    return results[0] if single and not save else tuple(results)


GROUPS = 4


def pack_kernel(cols, scal, *refs):
    vector_ref, out_ref = refs[4:6]
    for side in range(2):

        @pl.when(scal[0] % 2 == side)
        def _():
            for i in range(4):
                out_ref[:, i * cols : (i + 1) * cols] = refs[i][
                    :, side * cols : (side + 1) * cols
                ].astype(BF)

    vector = vector_ref[...].astype(BF)
    out_ref[:, 4 * cols :] = dot_rows(vector, unit_rows(vector.shape[0], 128)).astype(BF)


def pack_attention(scal, attention, vector, cols):
    rows = attention.shape[0]

    def pair(i):
        return pl.BlockSpec((rows, 2 * cols), lambda step, scal: (0, 2 * i + scal[0] // 2))

    return pl.pallas_call(
        functools.partial(pack_kernel, cols),
        out_shape=shaped((rows, 4 * cols + 128), BF),
        grid_spec=pltpu.PrefetchScalarGridSpec(
            num_scalar_prefetch=1,
            grid=(1,),
            in_specs=[pair(i) for i in range(4)] + [whole(*vector.shape)],
            out_specs=whole(rows, 4 * cols + 128),
        ),
        compiler_params=params(8),
        cost_estimate=cost(1.5),
        name="pack_attention",
    )(scal, *[attention] * 4, vector)


def cast_kernel(scal, in_ref, out_ref):
    out_ref[...] = in_ref[...].astype(BF)


def pack_forward(scal, forward, part):
    rows = forward.shape[0]
    return pl.pallas_call(
        cast_kernel,
        out_shape=shaped((rows, 2 * part), BF),
        grid_spec=pltpu.PrefetchScalarGridSpec(
            num_scalar_prefetch=1,
            grid=(2,),
            in_specs=[pl.BlockSpec((rows, part), lambda i, scal: (0, GROUPS * i + scal[0]))],
            out_specs=pl.BlockSpec((rows, part), lambda i, scal: (0, i)),
        ),
        compiler_params=params(8),
        cost_estimate=cost(1.5),
        name="pack_forward",
    )(scal, forward)


def place_rows(scal, pieces, target):
    rows = pieces[0].shape[0]
    if len(pieces) == 1:
        target[...] = pieces[0][...]
        return
    for i, piece in enumerate(pieces):
        start = pl.multiple_of(scal[1 + i] * rows, rows)
        target[pl.ds(start, rows), :] = piece[...]


def place_members(scal, pieces, target):
    rows = pieces[0].shape[0]
    for i, piece in enumerate(pieces):
        start = pl.multiple_of((scal[0] ^ i) * rows, rows)
        target[pl.ds(start, rows), :] = piece[...]


def place_kernel(scal, *refs):
    place_members(scal, refs[0:4], refs[4])


def place_blocks(scal, blocks):
    rows, width = blocks[0].shape
    wide = shaped((GROUPS * rows, width), BF)
    return run(place_kernel, "place_blocks", wide, (scal, *blocks), 0.5, mebibytes=2)


def project_kernel(count, cols, scal, seg_ref, x_ref, *refs):
    pieces = refs[:count]
    q_ref, k_ref, v_ref, wq_ref, wk_ref, wv_ref, wo_ref, vec_ref, col_ref = refs[count : 9 + count]
    weights = refs[9 + count]
    place_rows(scal, pieces, weights)
    for i, ref in enumerate((wq_ref, wk_ref, wv_ref, wo_ref)):
        ref[...] = weights[:, i * cols : (i + 1) * cols]
    unit = unit_rows(16, 128)
    vec_ref[...] = dot_cols(unit, weights[:, 4 * cols :])
    start = pl.multiple_of(scal[0] * cols, cols)
    own = dot_cols(unit, weights[pl.ds(start, cols), 4 * cols :])
    query_bias, value_bias = own[2:3, :], own[3:4, :]
    gain, shift = vec_ref[0:1, :], vec_ref[1:2, :]
    numbers = jnp.broadcast_to(seg_ref[...].astype(F32), (8, seg_ref.shape[1])).astype(BF)
    col_ref[...] = dot_rows(numbers, unit_rows(8, 128))[:, 0:1].astype(jnp.int32)
    block = 256

    def step(i, carry):
        rows = pl.ds(pl.multiple_of(i * block, block), block)
        hat, _ = normalize(x_ref[rows, :].astype(F32))
        normed = (hat * gain + shift).astype(BF)
        q_ref[rows, :] = (dot(normed, wq_ref[...]) + query_bias).astype(BF)
        k_ref[rows, :] = dot(normed, wk_ref[...]).astype(BF)
        v_ref[rows, :] = (dot(normed, wv_ref[...]) + value_bias).astype(BF)
        return carry

    lax.fori_loop(0, x_ref.shape[0] // block, step, 0)


def project(scal, segments, x_all, pieces, cols):
    length, width = x_all.shape
    outputs = (
        (shaped((length, cols), BF),) * 3
        + (shaped((width, cols), BF),) * 4
        + (shaped((16, width), F32), shaped((length, 1), jnp.int32))
    )
    return run(
        functools.partial(project_kernel, len(pieces), cols),
        "project",
        outputs,
        (scal, segments, x_all, *pieces),
        4.5,
        [pltpu.VMEM((width, 4 * cols + 128), BF)],
    )


def attend_kernel(per, first, scal, q_ref, k_ref, v_ref, seg_row_ref, seg_col_ref, *refs):
    out_ref = refs[-1]
    block = 256
    keys = k_ref[...]
    values = v_ref[...]

    def step(i, carry):
        start = pl.multiple_of(first + i * block, block)
        same = seg_col_ref[pl.ds(start, block), :] == seg_row_ref[...]
        queries = q_ref[pl.ds(start, block), :] * jnp.asarray(HEAD_DIM**-0.5, BF)
        result = jnp.zeros(queries.shape, F32)
        for head in range(per):
            lanes = head_lanes(head, queries.shape)
            score = dot_cols(jnp.where(lanes, queries, jnp.zeros_like(queries)), keys)
            score = jnp.where(same, score, masked_score)
            largest = jnp.max(score, axis=1, keepdims=True)
            power = jnp.exp(score - largest)
            total = jnp.sum(power, axis=1, keepdims=True)
            chance = (power * (1.0 / total)).astype(BF)
            result = jnp.where(lanes, dot(chance, values), result)
        out_ref[pl.ds(pl.multiple_of(i * block, block), block), :] = result.astype(BF)
        return carry

    lax.fori_loop(0, out_ref.shape[0] // block, step, 0)


def attend(scal, queries, keys, values, seg_row, seg_col, per, first, count, kept=()):
    inputs = (scal, queries, keys, values, seg_row, seg_col, *kept)
    return run(
        functools.partial(attend_kernel, per, first),
        "attend",
        shaped((count, queries.shape[1]), BF),
        inputs,
        7.0 * count / queries.shape[0],
        save=(1, 2, 3, 5, *range(6, len(inputs))) if kept else (),
    )


def forward_kernel(count, cols, parts, scal, x_ref, dy_ref, *refs):
    mixed, w_out = [refs[k * parts : (k + 1) * parts] for k in range(4)], refs[4 * parts :][:4]
    refs = refs[4 * parts + 4 :]
    pieces = refs[:count]
    vec_ref = refs[count]
    c_ref, u_ref, df_ref, keep_ref, send_ref, h_ref, w_ref, rows_ref, sums_ref = refs[
        1 + count : 10 + count
    ]
    out_weight = refs[10 + count]
    member = scal[0]
    part = w_ref.shape[1] // 2
    block = x_ref.shape[0] // GROUPS
    place_rows(scal, pieces, w_ref)
    for index in range(GROUPS):

        @pl.when(member == index)
        def _():
            for k in range(GROUPS):
                start = (index ^ k) * cols
                out_weight[:, start : start + cols] = w_out[k][...]

    rows_ref[...] = out_weight[pl.ds(pl.multiple_of(member * cols, cols), cols), :]
    zero = jnp.zeros((1, x_ref.shape[1]), F32)
    up_bias = vec_ref[pl.ds(8 + member, 1), :]

    def run_block(step, half, inner, carry):
        rows = pl.ds(pl.multiple_of(step * block, block), block)
        near = pl.ds(pl.multiple_of(inner * block, block), block)
        resid = x_ref[rows, :].astype(F32) + vec_ref[4:5, :]
        for k in range(GROUPS):
            start = pl.multiple_of((member ^ k) * cols, cols)
            resid += dot(mixed[k][half][near, :], out_weight[pl.ds(start, cols), :])

        @pl.when(step == member)
        def _():
            h_ref[...] = resid

        hat, _ = normalize(resid)
        normed = (hat * vec_ref[5:6, :] + vec_ref[6:7, :]).astype(BF)
        c_ref[rows, :] = normed
        pre = dot(normed, w_ref[:, :part]) + up_bias
        phi = 0.5 * (1.0 + lax.erf(pre * 0.7071067811865476))
        u_ref[rows, :] = (pre * phi).astype(BF)
        slope = phi + pre * (jnp.exp(-0.5 * pre * pre) * 0.3989422804014327)
        grad_pre = (dot(dy_ref[rows, :], w_ref[:, part:]) * slope).astype(BF)
        df_ref[rows, :] = grad_pre
        grad_normed = dot_cols(grad_pre, w_ref[:, :part])
        split_store(member, step, grad_normed, keep_ref, send_ref)
        return (
            carry[0] + jnp.sum(grad_normed * hat, axis=0, keepdims=True),
            carry[1] + jnp.sum(grad_normed, axis=0, keepdims=True),
            carry[2] + jnp.sum(grad_pre.astype(F32), axis=0, keepdims=True),
        )

    carry = (zero, zero, zero)
    inside = GROUPS // parts
    for half in range(parts):
        carry = lax.fori_loop(
            0,
            inside,
            lambda i, carry, half=half: run_block(half * inside + i, half, i, carry),
            carry,
        )
    sums_ref[...] = jnp.zeros_like(sums_ref)
    for i in range(3):
        sums_ref[i : i + 1, :] = carry[i]


def split_store(member, index, value, keep_ref, send_ref):
    mine = (index % 2) == (member % 2)

    @pl.when(mine)
    def _():
        keep_ref[index // 2] = value

    @pl.when(jnp.logical_not(mine))
    def _():
        send_ref[index // 2] = value.astype(BF)


def forward_back(scal, x_all, dy_all, mixed, w_out, pieces, vec, cols):
    length, width = x_all.shape
    part = pieces[0].shape[1] // 2
    rows = length // GROUPS
    outputs = (
        shaped((length, width), BF),
        shaped((length, part), BF),
        shaped((length, part), BF),
        shaped((2, rows, width), F32),
        shaped((2, rows, width), BF),
        shaped((rows, width), F32),
        shaped((width, 2 * part), BF),
        shaped((cols, width), BF),
        shaped((8, width), F32),
    )
    flat = [item for items in mixed for item in items]
    return run(
        functools.partial(forward_kernel, len(pieces), cols, len(mixed[0])),
        "forward_back",
        outputs,
        (scal, x_all, dy_all, *flat, *w_out, *pieces, vec),
        13.0,
        [pltpu.VMEM((width, width), BF)],
    )


def forward_grads_kernel(scal, c_ref, u_ref, df_ref, dy_ref, w_ref, *refs):
    own_ref, g_ref, keep_ref, send_ref = refs[-4:]
    part = u_ref.shape[1]
    block = u_ref.shape[0] // GROUPS
    third = c_ref.shape[1] // 3
    own_ref[...] = dy_ref[pl.ds(pl.multiple_of(scal[0] * block, block), block), :]

    def branch(i, carry):
        rows = pl.ds(pl.multiple_of(i * block, block), block)
        split_store(scal[0], i, dot_cols(u_ref[rows, :], w_ref[:, part:]), keep_ref, send_ref)
        return carry

    lax.fori_loop(0, GROUPS, branch, 0)

    def weight(i, carry):
        lanes = pl.ds(pl.multiple_of(i * third, third), third)
        g_ref[lanes, :part] = dot_rows(c_ref[:, lanes], df_ref[...]).astype(BF)
        g_ref[lanes, part:] = dot_rows(dy_ref[:, lanes], u_ref[...]).astype(BF)
        return carry

    lax.fori_loop(0, 3, weight, 0)


def forward_grads(scal, normed, active, grad_pre, dy_all, weights, kept):
    length, width = normed.shape
    part = active.shape[1]
    rows = length // GROUPS
    outputs = (
        shaped((rows, width), BF),
        shaped((width, 2 * part), BF),
        shaped((2, rows, width), F32),
        shaped((2, rows, width), BF),
    )
    inputs = (scal, normed, active, grad_pre, dy_all, weights, *kept)
    return run(
        forward_grads_kernel,
        "forward_grads",
        outputs,
        inputs,
        6.0,
        save=range(6, len(inputs)),
        far=(2,),
    )


def merge_kernel(scal, keep_ref, got_ref, mine_ref, send_ref):
    row = scal[0] // 2
    mine_ref[...] = keep_ref[row] + got_ref[row].astype(F32)
    send_ref[...] = (keep_ref[1 - row] + got_ref[1 - row].astype(F32)).astype(BF)


def merge(scal, keep, got, lazy=()):
    _, rows, width = keep.shape
    outputs = (shaped((rows, width), F32), shaped((rows, width), BF))
    return run(merge_kernel, "merge", outputs, (scal, keep, got), 0.7, mebibytes=8, lazy=lazy)


def resid_kernel(scal, mine_ref, got_ref, h_ref, dy_ref, vec_ref, dh_ref, dp_ref, sums_ref):
    grad = mine_ref[...] + got_ref[...].astype(F32)
    hat, inverse = normalize(h_ref[...])
    dy = dy_ref[...].astype(F32)
    grad_resid = dy + norm_back(hat, inverse, vec_ref[5:6, :], grad)
    dh_ref[...] = grad_resid
    low = grad_resid.astype(BF)
    dp_ref[...] = low
    sums_ref[...] = jnp.zeros_like(sums_ref)
    sums_ref[0:1, :] = jnp.sum(low.astype(F32), axis=0, keepdims=True)
    sums_ref[1:2, :] = jnp.sum(dy, axis=0, keepdims=True)


def resid_back(scal, mine, got, resid, cotangent, vec):
    rows, width = mine.shape
    outputs = (shaped((rows, width), F32), shaped((rows, width), BF), shaped((8, width), F32))
    return run(resid_kernel, "resid_back", outputs, (scal, mine, got, resid, cotangent, vec), 0.8)


def mixed_kernel(cols, parts, scal, *refs):
    grads, mixed = refs[0:4], [refs[4 + k * parts : 4 + (k + 1) * parts] for k in range(4)]
    rows_ref, do_ref, g_ref, all_ref, own_ref = refs[4 + 4 * parts :]
    share = all_ref.shape[0] // parts
    member = scal[0]
    place_members(scal, grads, all_ref)
    do_ref[...] = dot_cols(all_ref[...], rows_ref[...]).astype(BF)
    for index in range(GROUPS):

        @pl.when(member == index)
        def _():
            own_ref[...] = all_ref[:, index * cols : (index + 1) * cols]

    for k in range(GROUPS):
        start = pl.multiple_of((member ^ k) * cols, cols)
        total = dot_rows(mixed[k][0][...], own_ref[:share, :])
        for half in range(1, parts):
            total += dot_rows(mixed[k][half][...], own_ref[half * share : (half + 1) * share, :])
        g_ref[pl.ds(start, cols), :] = total.astype(BF)


def mixed_back(scal, grads, mixed, w_rows):
    rows, width = grads[0].shape
    cols = w_rows.shape[0]
    length = GROUPS * rows
    flat = [item for items in mixed for item in items]
    return run(
        functools.partial(mixed_kernel, cols, len(mixed[0])),
        "mixed_back",
        (shaped((length, cols), BF), shaped((width, cols), BF)),
        (scal, *grads, *flat, w_rows),
        2.5,
        [pltpu.VMEM((length, width), BF), pltpu.VMEM((length, cols), BF)],
        lazy=range(1 + GROUPS, 2 + GROUPS + len(flat)),
    )


def attend_back_kernel(
    per,
    scal,
    q_ref,
    k_ref,
    v_ref,
    do_ref,
    seg_row_ref,
    seg_col_ref,
    *refs,
):
    dq_ref, dk_ref, dv_ref, k_acc, v_acc = refs[-5:]
    block = 256
    k_acc[...] = jnp.zeros_like(k_acc)
    v_acc[...] = jnp.zeros_like(v_acc)
    keys = k_ref[...]
    values = v_ref[...]

    def step(i, carry):
        rows = pl.ds(pl.multiple_of(i * block, block), block)
        same = seg_col_ref[...] == seg_row_ref[:, rows]
        queries = q_ref[rows, :] * jnp.asarray(HEAD_DIM**-0.5, BF)
        grads = do_ref[rows, :]
        grad_query = jnp.zeros(queries.shape, F32)
        for head in range(per):
            lanes = head_lanes(head, queries.shape)
            query = jnp.where(lanes, queries, jnp.zeros_like(queries))
            grad = jnp.where(lanes, grads, jnp.zeros_like(grads))
            score = jnp.where(same, dot_cols(keys, query), masked_score)
            largest = jnp.max(score, axis=0, keepdims=True)
            power = jnp.exp(score - largest)
            total = jnp.sum(power, axis=0, keepdims=True)
            chance = power * (1.0 / total)
            grad_chance = dot_cols(values, grad)
            inner = jnp.sum(chance * grad_chance, axis=0, keepdims=True)
            grad_score = (chance * (grad_chance - inner)).astype(BF)
            k_acc[...] += dot(grad_score, query)
            v_acc[...] += dot(chance.astype(BF), grad)
            grad_query = jnp.where(lanes, dot_rows(grad_score, keys), grad_query)
        dq_ref[rows, :] = (grad_query * HEAD_DIM**-0.5).astype(BF)
        return carry

    lax.fori_loop(0, q_ref.shape[0] // block, step, 0)
    dk_ref[...] = k_acc[...].astype(BF)
    dv_ref[...] = v_acc[...].astype(BF)


def attend_back(scal, queries, keys, values, grad_out, seg_row, seg_col, per, kept):
    shape = shaped(queries.shape, BF)
    wide = pltpu.VMEM(queries.shape, F32)
    inputs = (scal, queries, keys, values, grad_out, seg_row, seg_col, *kept)
    return run(
        functools.partial(attend_back_kernel, per),
        "attend_back",
        (shape, shape, shape),
        inputs,
        16.0,
        [wide, wide],
        lazy=(1, 2, 3, 6),
        save=range(7, len(inputs)),
    )


def project_back_kernel(cols, scal, *refs):
    x_ref = refs[0]
    grads, weights = refs[1:4], refs[4:7]
    vec_ref, forward_ref, resid_ref, out_ref = refs[7:11]
    g_ref, keep_ref, send_ref, rows_ref, a_ref = refs[11:16]
    member = scal[0]
    block = 256
    width = x_ref.shape[1]
    zero = jnp.zeros((1, width), F32)

    g_ref[:, 3 * cols : 4 * cols] = out_ref[...]

    def step(i, carry):
        rows = pl.ds(pl.multiple_of(i * block, block), block)
        hat, _ = normalize(x_ref[rows, :].astype(F32))
        a_ref[rows, :] = (hat * vec_ref[0:1, :] + vec_ref[1:2, :]).astype(BF)
        grad = dot_cols(grads[0][rows, :], weights[0][...])
        grad += dot_cols(grads[1][rows, :], weights[1][...])
        grad += dot_cols(grads[2][rows, :], weights[2][...])
        split_store(member, i, grad, keep_ref, send_ref)
        return (
            carry[0] + jnp.sum(grad * hat, axis=0, keepdims=True),
            carry[1] + jnp.sum(grad, axis=0, keepdims=True),
        )

    gain, shift = lax.fori_loop(0, GROUPS, step, (zero, zero))
    for i in range(3):
        g_ref[:, i * cols : (i + 1) * cols] = dot_rows(a_ref[...], grads[i][...]).astype(BF)
    rows_ref[...] = jnp.zeros_like(rows_ref)
    listed = (gain, shift, None, None, resid_ref[0:1, :], forward_ref[0:1, :], forward_ref[1:2, :])
    listed += (resid_ref[1:2, :],)
    for i, row in enumerate(listed):
        if row is not None:
            rows_ref[i : i + 1, :] = row
    rows_ref[pl.ds(8 + member, 1), :] = forward_ref[2:3, :]
    rows = rows_ref[...]
    high = rows.astype(BF)
    low = (rows - high.astype(F32)).astype(BF)
    unit = unit_rows(16, 128)
    shifted = jnp.where(
        lax.broadcasted_iota(jnp.int32, (16, 128), 1)
        == lax.broadcasted_iota(jnp.int32, (16, 128), 0) + 16,
        1.0,
        0.0,
    ).astype(BF)
    table = dot_rows(high, unit) + dot_rows(low, shifted)
    lane = lax.broadcasted_iota(jnp.int32, (cols, 128), 1)
    bias = jnp.zeros((cols, 128), F32)
    ones = jnp.ones((grads[0].shape[0], 8), BF)
    for i, column in ((0, 2), (2, 3)):
        total = dot_rows(grads[i][...], ones)[:, 0:1]
        top = total.astype(BF).astype(F32)
        bias = jnp.where(lane == column, top, bias)
        bias = jnp.where(lane == column + 16, total - top, bias)
    g_ref[:, 4 * cols :] = table.astype(BF)
    own = pl.ds(pl.multiple_of(member * cols, cols), cols)
    g_ref[own, 4 * cols :] = (g_ref[own, 4 * cols :].astype(F32) + bias).astype(BF)


def project_back(scal, x_all, grads, weights, vec, sums_forward, sums_resid, grad_out):
    length, width = x_all.shape
    cols = grads[0].shape[1]
    rows = length // GROUPS
    return run(
        functools.partial(project_back_kernel, cols),
        "project_back",
        (
            shaped((width, 4 * cols + 128), BF),
            shaped((2, rows, width), F32),
            shaped((2, rows, width), BF),
        ),
        (scal, x_all, *grads, *weights, vec, sums_forward, sums_resid, grad_out),
        5.0,
        [pltpu.VMEM((16, width), F32), pltpu.VMEM((length, width), BF)],
        lazy=(1, *range(5, 12)),
    )


def input_kernel(scal, mine_ref, got_ref, x_ref, dh_ref, vec_ref, out_ref):
    grad = mine_ref[...] + got_ref[...].astype(F32)
    hat, inverse = normalize(x_ref[...].astype(F32))
    out_ref[...] = dh_ref[...] + norm_back(hat, inverse, vec_ref[0:1, :], grad)


def input_back(scal, mine, got, tokens, grad_resid, vec):
    inputs = (scal, mine, got, tokens, grad_resid, vec)
    return run(input_kernel, "input_back", shaped(mine.shape, F32), inputs, 1.0, lazy=(3, 4, 5))


def output_kernel(scal, mine_ref, got_ref, h_ref, vec_ref, out_ref):
    branch = mine_ref[...] + got_ref[...].astype(F32) + vec_ref[7:8, :]
    out_ref[...] = (h_ref[...] + branch).astype(BF)


def output_sum(scal, mine, got, resid, vec):
    inputs = (scal, mine, got, resid, vec)
    return run(output_kernel, "output_sum", shaped(mine.shape, BF), inputs, 0.8, lazy=(3, 4))


def owned_kernel(scal, in_ref, low_ref, squares_ref):
    total = in_ref[0].astype(F32)
    for i in range(1, in_ref.shape[0]):
        total += in_ref[i].astype(F32)
    low = total.astype(BF)
    low_ref[...] = low
    wide = low.astype(F32)
    squares_ref[...] = jnp.full(squares_ref.shape, jnp.sum(wide * wide), F32)


def owned_sum(scal, pieces):
    outputs = (shaped(pieces.shape[1:], BF), shaped((8, 128), F32))
    return run(owned_kernel, "owned_sum", outputs, (scal, pieces), 1.5, lazy=(1,))


def owned_vector_kernel(cols, scal, in_ref, low_ref):
    total = in_ref[0].astype(F32)
    for i in range(1, in_ref.shape[0]):
        total += in_ref[i].astype(F32)
    low_ref[:, : 4 * cols] = total[:, : 4 * cols].astype(BF)
    vector = total[:, 4 * cols :]
    low_ref[:, 4 * cols : 4 * cols + 128] = vector.astype(BF)
    low_ref[:, 4 * cols + 128 :] = (vector - vector.astype(BF).astype(F32)).astype(BF)


def owned_vector(scal, pieces, cols):
    _, rows, width = pieces.shape
    return run(
        functools.partial(owned_vector_kernel, cols),
        "owned_vector",
        shaped((rows, width + 128), BF),
        (scal, pieces),
        1.5,
    )


def join_kernel(cols, count, scal, *refs):
    pieces, squares = refs[0:4], refs[4:8]
    gradient_ref, vector_ref, squares_ref = refs[8:11]
    width = gradient_ref.shape[1] // 4
    for member in range(GROUPS):

        @pl.when(scal[0] == member)
        def _():
            for i in range(4):
                for k in range(GROUPS):
                    start = i * width + (member ^ k) * cols
                    gradient_ref[:, start : start + cols] = pieces[k][
                        :, i * cols : (i + 1) * cols
                    ].astype(F32)

    def vector_of(piece):
        high = piece[:, 4 * cols : 4 * cols + 128].astype(F32)
        return high + piece[:, 4 * cols + 128 :].astype(F32)

    halves = [vector_of(piece) for piece in pieces]
    table = (halves[0] + halves[1]) + (halves[2] + halves[3])
    rows = lax.broadcasted_iota(jnp.int32, (16, 128), 0)
    lanes = lax.broadcasted_iota(jnp.int32, (16, 128), 1)
    unit = jnp.where((lanes == rows) | (lanes == rows + 16), 1.0, 0.0)
    vector = lax.dot_general(
        unit,
        table,
        (((1,), (1,)), ((), ())),
        preferred_element_type=F32,
        precision=lax.Precision.HIGHEST,
    )[:count]
    vector_ref[...] = vector
    gradient = gradient_ref[...]
    total = jnp.sum(gradient * gradient) + jnp.sum(vector * vector)
    forward = (squares[0][...] + squares[1][...]) + (squares[2][...] + squares[3][...])
    squares_ref[...] = forward + total


def join(scal, pieces, squares, width, count, cols):
    rows = pieces[0].shape[0]
    return run(
        functools.partial(join_kernel, cols, count),
        "join",
        (shaped((rows, 4 * width), F32), shaped((count, rows), F32), shaped((8, 128), F32)),
        (scal, *pieces, *squares),
        1.5,
    )


def clip_factor(total_ref):
    total = total_ref[0]
    for i in range(1, total_ref.shape[0]):
        total += total_ref[i]
    norm = jnp.sqrt(total[0:1, 0:1])
    return jnp.minimum(1.0, clip_limit / (norm + 1e-06))


def adam_kernel(counts, scal, total_ref, attention_ref, vector_ref, *refs):
    grads = refs[0:4]
    sources, targets = refs[4:16], refs[16:31]
    held, copies = refs[31:43], refs[43:46]
    loads, stores = refs[46:49], refs[49:52]
    factor = clip_factor(total_ref)
    decays = (weight_decay, weight_decay, 0.0)

    def chunk(kind, i):
        if counts[kind] == 1:
            return (slice(None), slice(None))
        size = held[4 * kind].shape[1] // counts[kind]
        return (slice(None), pl.ds(pl.multiple_of(i * size, size), size))

    def load(kind, i, state):
        place = chunk(kind, i)
        number = 4 * kind + state
        return pltpu.make_async_copy(
            sources[number].at[place], held[number].at[place], loads[kind].at[i, state]
        )

    def store(kind, i, state):
        place = chunk(kind, i)
        source = held[4 * kind + state] if state < 4 else copies[kind]
        return pltpu.make_async_copy(
            source.at[place], targets[3 * state + kind].at[place], stores[kind].at[i, state]
        )

    def every(kind, action):
        def step(i, carry):
            action(kind, i)
            return carry

        lax.fori_loop(0, counts[kind], step, 0)

    def start(kind, i):
        for state in range(4):
            load(kind, i, state).start()

    def work(kind, i):
        for state in range(4):
            load(kind, i, state).wait()
        place = chunk(kind, i)
        if kind == 0:
            gradient = attention_ref[place]
        elif kind == 2:
            gradient = vector_ref[...]
        else:
            size = held[4].shape[1] // counts[1]
            half = pl.ds(pl.multiple_of((i // GROUPS) * size, size), size)
            source = scal[0] ^ (i % GROUPS)
            gradient = grads[0][:, half]
            for k in range(1, GROUPS):
                gradient = jnp.where(source == k, grads[k][:, half], gradient)
            gradient = gradient.astype(F32)
        results = adam_update(
            *[held[4 * kind + state][place] for state in range(4)], gradient, factor, decays[kind]
        )
        for state, value in zip((0, 1, 2, 3), results):
            held[4 * kind + state][place] = value
        copies[kind][place] = results[0].astype(BF)
        for state in range(5):
            store(kind, i, state).start()

    def finish(kind, i):
        for state in range(5):
            store(kind, i, state).wait()

    for kind in (1, 0, 2):
        every(kind, start)
    for kind in (1, 0, 2):
        every(kind, work)
    for kind in (1, 0, 2):
        every(kind, finish)


def adam(scal, totals, attention_grad, vector_grad, forward_grads_by_member, states):
    counts = (4, 2 * GROUPS, 1)
    kinds = [states[4 * kind].shape for kind in range(3)]
    out_shape = [pltpu.HBM(shape, F32) for _ in range(4) for shape in kinds]
    out_shape += [pltpu.HBM(shape, BF) for shape in kinds]
    return pl.pallas_call(
        functools.partial(adam_kernel, counts),
        out_shape=out_shape,
        in_specs=[smem()] + [vmem()] * 7 + [far_space()] * 12,
        out_specs=[far_space()] * 15,
        scratch_shapes=[pltpu.VMEM(kinds[kind], F32) for kind in range(3) for _ in range(4)]
        + [pltpu.VMEM(shape, BF) for shape in kinds]
        + [pltpu.SemaphoreType.DMA((count, 4)) for count in counts]
        + [pltpu.SemaphoreType.DMA((count, 5)) for count in counts],
        compiler_params=params(32),
        cost_estimate=cost(9.0),
        name="adam",
    )(scal, totals, attention_grad, vector_grad, *forward_grads_by_member, *map(pin, states))


def adam_update(master, moment, second, teacher, gradient, factor, decay_rate):
    clipped = gradient * factor
    moment_new = beta_one * moment + (1.0 - beta_one) * clipped
    second_new = beta_two * second + (1.0 - beta_two) * clipped * clipped
    scale_one = 1.0 - beta_one**ADAM_STEP
    scale_two = 1.0 - beta_two**ADAM_STEP
    update = (moment_new * (1.0 / scale_one)) / (
        jnp.sqrt(second_new * (1.0 / scale_two)) + adam_epsilon
    )
    master_new = master * (1.0 - learn_rate * decay_rate) - learn_rate * update
    teacher_new = teacher_keep * teacher + (1.0 - teacher_keep) * master_new
    return (master_new, moment_new, second_new, teacher_new)


def swap(part, bit):
    return lax.ppermute(part, "head", [(i, i ^ bit) for i in range(4)])


def spread(part, *others):
    across = swap(part, 2)
    if others:
        return [
            part,
            swap(after(part, *others), 1),
            across,
            swap(after(across, *others), 1),
        ]
    return [part, swap(part, 1), across, swap(across, 1)]


RING = (0, 2, 4, 6, 7, 5, 3, 1)


def ring_owners(count):
    if count != len(RING):
        return np.zeros((count, 1), np.int32)
    table = []
    for device in range(count):
        place = RING.index(device)
        owners = [device]
        for hop in range(1, count // 2 + 1):
            owners.append(RING[(place - hop) % count])
            if hop < count // 2:
                owners.append(RING[(place + hop) % count])
        table.append(owners)
    return np.asarray(table, np.int32)


def after(value, *others):
    return lax.optimization_barrier((value, *others))[0]


class Ring:
    def __init__(self, block, count):
        self.count = count
        self.hops = count // 2 if count == len(RING) else 1
        self.front = self.rear = block
        self.pieces = [block]
        self.done = 0

    def hop(self, *others):
        self.done += 1
        if self.count != len(RING):
            self.pieces = [lax.all_gather(after(self.front, *others), "dp", axis=0, tiled=True)]
            return self
        ahead = [(RING[i], RING[(i + 1) % self.count]) for i in range(self.count)]
        back = [(target, source) for source, target in ahead]
        last = self.done == self.hops
        if self.done > 1 or others:
            self.front, self.rear = lax.optimization_barrier((self.front, self.rear, *others))[:2]
        self.front = lax.ppermute(self.front, "dp", ahead)
        self.pieces.append(self.front)
        if not last:
            self.rear = lax.ppermute(self.rear, "dp", back)
            self.pieces.append(self.rear)
        return self

    def rest(self):
        while self.done < self.hops:
            self.hop()
        return self.pieces


def exchange_owned(grads, count):
    blocks = grads.reshape(count, -1, grads.shape[1])
    return lax.all_to_all(blocks, "dp", split_axis=0, concat_axis=0)


def local(
    tokens,
    cotangent,
    segments,
    attention_master,
    feedforward_master,
    vector_master,
    attention_moment,
    feedforward_moment,
    vector_moment,
    attention_second,
    feedforward_second,
    vector_second,
    attention_teacher,
    feedforward_teacher,
    vector_teacher,
):
    width = tokens.shape[1]
    owners = lax.axis_size("dp")
    groups = lax.axis_size("head")
    hidden = feedforward_master.shape[1] // 2
    per = HEADS // groups
    cols = per * HEAD_DIM
    part = hidden // groups

    owner_table = ring_owners(owners)
    table = np.concatenate(
        [
            np.tile(np.arange(groups, dtype=np.int32), owners)[:, None],
            np.repeat(owner_table, groups, axis=0),
        ],
        axis=1,
    )
    place = lax.axis_index("dp") * groups + lax.axis_index("head")
    scal = lax.dynamic_index_in_dim(jnp.asarray(table), place, 0, keepdims=False)
    first = Ring(pack_attention(scal, attention_master, vector_master, cols), owners)
    first.rest()
    early = first.pieces[-2] if owners == len(RING) else first.pieces[0]
    middle = first.pieces[3] if owners == len(RING) else first.pieces[0]
    x_all = place_blocks(scal, spread(tokens, early))
    second = Ring(pack_forward(scal, feedforward_master, part), owners)
    second.hop(early)
    across = swap(after(cotangent, middle), 2)

    queries, keys, values, w_q, w_k, w_v, w_o, vec, seg_col = project(
        scal, segments, x_all, first.pieces, cols
    )
    if second.done < second.hops:
        second.hop(queries)
    half = x_all.shape[0] // 2
    w_across = swap(w_o, 2)
    mixed_low, *kept = attend(
        scal,
        queries,
        keys,
        values,
        segments,
        seg_col,
        per,
        0,
        half,
        (x_all, w_q, w_k, w_v, vec),
    )
    far_q, far_k, far_v, far_col, far_x, far_wq, far_wk, far_wv, far_vec = kept
    low_across = swap(mixed_low, 2)
    w_across = after(w_across, mixed_low)
    if second.done < second.hops:
        second.hop(mixed_low)
    mixed_high = attend(
        scal, after(queries, w_across), keys, values, segments, seg_col, per, half, half
    )
    high_across = swap(mixed_high, 2)
    across, w_across, low_across, w_o, mixed_low, cot = lax.optimization_barrier(
        (across, w_across, low_across, w_o, mixed_low, cotangent, high_across)
    )[:6]
    dy_all = place_blocks(scal, [cot, swap(cot, 1), across, swap(across, 1)])
    w_out = [w_o, swap(w_o, 1), w_across, swap(w_across, 1)]
    mixed = [
        (mixed_low, mixed_high),
        (swap(mixed_low, 1), swap(mixed_high, 1)),
        (low_across, high_across),
        (swap(low_across, 1), swap(high_across, 1)),
    ]
    normed_two, active, grad_pre, keep, send, resid, w_ff, w_rows, sums_forward = forward_back(
        scal, x_all, dy_all, mixed, w_out, second.rest(), vec, cols
    )
    mine, send = merge(scal, keep, swap(send, 1))
    flat = [item for items in mixed for item in items]
    cot_own, grad_ff, keep_branch, send_branch, *kept = forward_grads(
        scal,
        after(normed_two, send),
        active,
        grad_pre,
        dy_all,
        w_ff,
        (resid, sums_forward, w_rows, *flat),
    )
    far_resid, far_sums, far_rows = kept[:3]
    far_mixed = [tuple(kept[3 + 2 * k : 5 + 2 * k]) for k in range(GROUPS)]
    grad_resid, grad_low, sums_resid = resid_back(scal, mine, swap(send, 2), resid, cot_own, vec)
    low_blocks = spread(grad_low)
    owned_ff = exchange_owned(after(grad_ff, low_blocks[1]), owners)
    grad_mixed, grad_out = mixed_back(scal, low_blocks, far_mixed, far_rows)
    mine, send = merge(
        scal, keep_branch, swap(after(send_branch, low_blocks[1]), 1), lazy=(1,)
    )
    *grad_qkv, far_dh, far_sums_resid, far_grad_out = attend_back(
        scal,
        far_q,
        far_k,
        far_v,
        grad_mixed,
        segments,
        far_col,
        per,
        (grad_resid, sums_resid, grad_out),
    )
    block_output = output_sum(scal, mine, swap(send, 2), far_resid, far_vec)
    pack, keep, send = project_back(
        scal,
        far_x,
        grad_qkv,
        (far_wq, far_wk, far_wv),
        far_vec,
        far_sums,
        far_sums_resid,
        far_grad_out,
    )
    owned_pack = exchange_owned(pack, owners)
    mine, send = merge(scal, keep, swap(send, 1))
    input_gradient = input_back(scal, mine, swap(send, 2), tokens, far_dh, far_vec)
    sum_ff, squares_ff = owned_sum(scal, after(owned_ff, pack))
    forward_parts = spread(sum_ff)
    forward_squares = spread(squares_ff)
    owned_pack = after(
        owned_pack, input_gradient, block_output, *forward_parts, *forward_squares
    )
    attention_parts = spread(owned_vector(scal, owned_pack, cols))
    attention_grad, vector_grad, squares = join(
        scal, attention_parts, forward_squares, width, vector_master.shape[0], cols
    )
    totals = lax.all_to_all(
        jnp.broadcast_to(squares, (owners, 8, 128)), "dp", split_axis=0, concat_axis=0
    )
    gradient_norm = jnp.sqrt(jnp.sum(totals[:, 0, 0]))
    results = adam(
        scal,
        totals,
        attention_grad,
        vector_grad,
        forward_parts,
        (
            attention_master,
            attention_moment,
            attention_second,
            attention_teacher,
            feedforward_master,
            feedforward_moment,
            feedforward_second,
            feedforward_teacher,
            vector_master,
            vector_moment,
            vector_second,
            vector_teacher,
        ),
    )
    return (block_output, input_gradient, gradient_norm, *results)


def solution(mesh):
    rows = P(("dp", "head"), None)
    shard = P("dp", None)
    vector = P(None, "dp")
    return jax.shard_map(
        local,
        mesh=mesh,
        in_specs=(rows, rows, shard) + (shard, shard, vector) * 4,
        out_specs=(rows, rows, P()) + (shard, shard, vector) * 5,
        check_vma=False,
    )
```

time: 475 us -> 254 us (0.53); the launches traced: 469 us -> 253 us
  blocking collectives: 137 us -> 12.4 us
  local copies, waits for them, and re-layouts: 78.5 us -> 4.65 us
  Pallas kernels: 24.6 us -> 93.4 us
  other arithmetic: 42.5 us -> 0.61 us
  starting transfers between devices: 12.6 us -> 48.1 us
  matrix products: 32 us -> 0 us
  waiting for transfers between devices: 122 us -> 91.1 us
  between operations: 19.4 us -> 2.81 us
    all_gather x11 -> x0, blocking collectives: 137 us -> none  [the longest x7 67.6 us: gather_head(): rows = lax.all_gather(part, 'head', axis=0, axis_index_groups=PAIR_ROW)]
    all_gather x6 -> x0, waiting for transfers between devices: 72.3 us -> none  [the longest x1 66.5 us: local(): w_rest = lax.all_gather(low_rest, 'dp', axis=0, tiled=True)]
    pallas_call x2 -> x22, Pallas kernels: 24.6 us -> 93.4 us  [the longest x19 79.2 us: run(): pl.pallas_call(body, out_shape=shapes + [pltpu.HBM(inputs[i].shape, input...]
    ppermute x6 -> x33, waiting for transfers between devices: 17.3 us -> 56.3 us  [swap(): return lax.ppermute(part, 'head', [(i, i ^ bit) for i in range(4)])]
    dot_general x12 -> x0, matrix products: 32 us -> none  [the longest x4 12.2 us: dot(): return jnp.dot(left, right, preferred_element_type=F32)]
    ppermute x0 -> x14, waiting for transfers between devices: none -> 26.3 us  [the longest x8 19.7 us: hop(): self.front = lax.ppermute(self.front, 'dp', ahead)]
    all_to_all x2, waiting for transfers between devices: 32.3 us -> 8.5 us  [exchange_owned(): return lax.all_to_all(blocks, 'dp', split_axis=0, concat_axis=0)]
    unnamed x167 -> x18, local copies, waits for them, and re-layouts: 25.5 us -> 3.94 us
  transfers between devices with their start and end apart: 15 -> 49, of which waited for: 6 -> 27; matrix products, arithmetic and copies ran while one was open for 22% -> 0% of each run, Pallas kernels for 5% -> 26%
where the time goes in v2:
time: 254 us; the launch traced here: 253 us
  Pallas kernels  93.4 us (37%)
  waiting for transfers between devices  91.1 us (36%)
  starting transfers between devices  48.1 us (19%)
  blocking collectives  12.4 us (5%)
  local copies, waits for them, and re-layouts  4.65 us (2%)
  between operations  2.81 us (1%)
    pallas_call x19, Pallas kernels, run(): pl.pallas_call(body, out_shape=shapes + [pltpu.HBM(inputs[i].shape, input...  79.2 us
    ppermute x33, waiting for transfers between devices, swap(): return lax.ppermute(part, 'head', [(i, i ^ bit) for i in range(4)])  56.3 us
    ppermute x33, starting transfers between devices, swap(): return lax.ppermute(part, 'head', [(i, i ^ bit) for i in range(4)])  20.7 us
    ppermute x8, waiting for transfers between devices, hop(): self.front = lax.ppermute(self.front, 'dp', ahead)  19.7 us
    pallas_call x1, Pallas kernels, adam(): pl.pallas_call(functools.partial(adam_kernel, counts), out_shape=out_shap...  12.6 us
    all_to_all x1, blocking collectives, local(): lax.all_to_all(jnp.broadcast_to(squares, (owners, 8, 128)), 'dp', split_a...  12.4 us
    ppermute x8, starting transfers between devices, hop(): self.front = lax.ppermute(self.front, 'dp', ahead)  10.4 us
    all_to_all x2, starting transfers between devices, exchange_owned(): return lax.all_to_all(blocks, 'dp', split_axis=0, concat_axis=0)  9.5 us
  transfers between devices with their start and end apart: 49, of which 27 were waited for; matrix products, arithmetic and copies ran while one was open for 0% of the time, Pallas kernels for 26%

profile of v2, /device:TPU:0, one launch (start us, length us, event | category | flops | bytes accessed | tf_op | source)
XLA Modules:
  0.0 253.0 jit_solution(14725372227127299950)
XLA Ops:
  1.4 1.3 copy-done
  3.3 0.9 pack_attention.1.refs_3_
  4.2 3.0 %collective-permute-start.1 = (bf16[96,896]{1,0:T(8,128)(2,1)S(1)}, bf16[96,896]{1,0:T(8,128)(2,1)S(1)}, u32[]{:S(2)}, u32[]{:S(2)}) collective-permute-start(bf16[96,896]{1,0:T(8,128)(2,1)S(1)} %pack_attention.1.refs_3_), channel_id=1, source_target_pairs={{8,0},{16,8},{24,16},{28,24},{20,28},{12,20},{4,12},{0,4},{9,1},{1... | collective-permute-start | bytes 516104 | tf_op jit(solution)/shard_map/ppermute | solution.py:976
  7.4 1.9 collective-permute-start.6
  9.3 2.4 collective-permute-done.1.refs_5_
  11.7 1.4 collective-permute-done.refs_4_
  13.5 1.6 collective-permute-start.3
  15.1 3.4 %collective-permute-done.2.refs_6_ = bf16[96,896]{1,0:T(8,128)(2,1)S(1)} collective-permute-done((bf16[96,896]{1,0:T(8,128)(2,1)S(1)}, bf16[96,896]{1,0:T(8,128)(2,1)S(1)}, u32[]{:S(2)}, u32[]{:S(2)}) %collective-permute-start.2) | collective-permute-done | bytes 172064 | tf_op jit(solution)/shard_map/ppermute | solution.py:973
  18.9 1.6 collective-permute-start.4
  20.5 3.8 %collective-permute-done.4.refs_9_ = bf16[96,896]{1,0:T(8,128)(2,1)S(1)} collective-permute-done((bf16[96,896]{1,0:T(8,128)(2,1)S(1)}, bf16[96,896]{1,0:T(8,128)(2,1)S(1)}, u32[]{:S(2)}, u32[]{:S(2)}) %collective-permute-start.4) | collective-permute-done | bytes 172064 | tf_op jit(solution)/shard_map/ppermute | solution.py:976
  24.8 1.7 collective-permute-start.9
  27.2 1.6 collective-permute-start.22
  29.3 2.7 %collective-permute-done.9.refs_8_ = bf16[96,896]{1,0:T(8,128)(2,1)S(1)} collective-permute-done((bf16[96,896]{1,0:T(8,128)(2,1)S(1)}, bf16[96,896]{1,0:T(8,128)(2,1)S(1)}, u32[]{:S(2)}, u32[]{:S(2)}) %collective-permute-start.9) | collective-permute-done | bytes 172064 | tf_op jit(solution)/shard_map/ppermute | solution.py:973
  32.0 1.7 collective-permute-start.10
  34.4 6.7 %collective-permute-done.10.refs_10_ = bf16[96,896]{1,0:T(8,128)(2,1)S(1)} collective-permute-done((bf16[96,896]{1,0:T(8,128)(2,1)S(1)}, bf16[96,896]{1,0:T(8,128)(2,1)S(1)}, u32[]{:S(2)}, u32[]{:S(2)}) %collective-permute-start.10) | collective-permute-done | bytes 172064 | tf_op jit(solution)/shard_map/ppermute | solution.py:973
  41.1 3.9 %project.1 = (bf16[1024,192]{1,0:T(8,128)(2,1)S(1)}, bf16[1024,192]{1,0:T(8,128)(2,1)S(1)}, bf16[1024,192]{1,0:T(8,128)(2,1)S(1)}, bf16[768,192]{1,0:T(8,128)(2,...) custom-call(s32[9]{0:T(128)S(1)} %dynamic-slice_bitcast_fusion.scal., ...), custom_call_target="tpu_custom_call" | custom-call | bytes 16200000 | tf_op jit(solution)/shard_map/project/pallas_call | solution.py:148
  45.0 1.7 collective-permute-start.11
  46.7 1.6 collective-permute-start.24
  49.1 4.3 %attend.2 = (bf16[512,192]{1,0:T(8,128)(2,1)S(1)}, bf16[1024,192]{1,0:T(8,128)(2,1)}, bf16[1024,192]{1,0:T(8,128)(2,1)}, bf16[1024,192]{1,0:T(8,128)(2,1)}, s32[...) custom-call(s32[9]{0:T(128)S(1)} %dynamic-slice_bitcast_fusion.scal., ...), custom_call_target="tpu_custom_call" | custom-call | bytes 12600000 | tf_op jit(solution)/shard_map/attend/pallas_call | solution.py:148
  53.5 1.7 collective-permute-start.12
  55.1 2.0 collective-permute-done.11.refs_13_
  57.1 4.2 %attend.3.refs_4_.refs_10_ = bf16[512,192]{1,0:T(8,128)(2,1)S(1)} custom-call(s32[9]{0:T(128)S(1)} %dynamic-slice_bitcast_fusion.scal.refs_0_, bf16[1024,192]{1,0:T(8,128)(2,1)S(1)} %get-tuple-element.148.refs_1_, bf16[1024,192]{1,0:T(8,128)(2,1)S(1)} %get-tuple-element.139.refs_2_, bf16[1024,192]{1,0:T(8,128)(2,1)S(1)} %get-tuple-element.140.refs_3_, ...), custom_call_target="tpu_custom_call" | custom-call | bytes 12600000 | tf_op jit(solution)/shard_map/attend/pallas_call | solution.py:148
  61.3 1.7 collective-permute-start.13
  63.0 1.6 collective-permute-start.26
  65.5 5.6 %collective-permute-done.12.refs_7_.refs_13_ = bf16[512,192]{1,0:T(8,128)(2,1)S(1)} collective-permute-done((bf16[512,192]{1,0:T(8,128)(2,1)S(1)}, bf16[512,192]{1,0:T(8,128)(2,1)S(1)}, u32[]{:S(2)}, u32[]{:S(2)}) %collective-permute-start.12) | collective-permute-done | bytes 196640 | tf_op jit(solution)/shard_map/ppermute | solution.py:918
  71.2 3.7 %collective-permute-done.13.refs_8_.refs_14_ = bf16[512,192]{1,0:T(8,128)(2,1)S(1)} collective-permute-done((bf16[512,192]{1,0:T(8,128)(2,1)S(1)}, bf16[512,192]{1,0:T(8,128)(2,1)S(1)}, u32[]{:S(2)}, u32[]{:S(2)}) %collective-permute-start.13) | collective-permute-done | bytes 196640 | tf_op jit(solution)/shard_map/ppermute | solution.py:918
  76.0 1.6 collective-permute-done.17.refs_6_.refs_12_
  77.9 1.7 collective-permute-start.28
  81.5 5.5 %collective-permute-done.28.refs_22_ = bf16[96,1536]{1,0:T(8,128)(2,1)S(1)} collective-permute-done((bf16[96,1536]{1,0:T(8,128)(2,1)S(1)}, bf16[96,1536]{1,0:T(8,128)(2,1)S(1)}, u32[]{:S(2)}, u32[]{:S(2)}) %collective-permute-start.28) | collective-permute-done | bytes 294944 | tf_op jit(solution)/shard_map/ppermute | solution.py:973
  87.0 11.3 %forward_back.1 = (bf16[1024,768]{1,0:T(8,128)(2,1)S(1)}, bf16[1024,768]{1,0:T(8,128)(2,1)S(1)}, bf16[1024,768]{1,0:T(8,128)(2,1)S(1)}, f32[2,256,768]{2,1,0:T(8...) custom-call(s32[9]{0:T(128)S(1)} %dynamic-slice_bitcast_fusion.scal., ...), custom_call_target="tpu_custom_call" | custom-call | bytes 46800000 | tf_op jit(solution)/shard_map/forward_back/pallas_call | solution.py:148
  98.3 2.3 collective-permute-done.29.refs_2_
  101.3 1.7 collective-permute-start.30
  103.0 7.5 %forward_grads.1 = (bf16[256,768]{1,0:T(8,128)(2,1)S(1)}, bf16[768,1536]{1,0:T(8,128)(2,1)}, f32[2,256,768]{2,1,0:T(8,128)}, bf16[2,256,768]{2,1,0:T(8,128)(2,1)...) custom-call(s32[9]{0:T(128)S(1)} %dynamic-slice_bitcast_fusion.scal., ...), custom_call_target="tpu_custom_call" | custom-call | bytes 21600000 | tf_op jit(solution)/shard_map/forward_grads/pallas_call | solution.py:148
  110.5 2.0 collective-permute-done.30.refs_2_
  112.5 1.2 resid_back.1
  113.8 1.7 collective-permute-done.31.refs_2_
  115.5 5.9 %all-to-all-start.1 = ((bf16[8,96,1536]{2,1,0:T(8,128)(2,1)}), bf16[8,96,1536]{2,1,0:T(8,128)(2,1)}, u32[]{:S(2)}, u32[]{:S(2)}) async-start(bf16[8,96,1536]{2,1,0:T(8,128)(2,1)} %bitcast.2), calls=%async_computation.1 | async-start | bytes 4718592 | tf_op jit(solution)/shard_map/all_to_all | solution.py:988
  121.4 1.5 collective-permute-start.34
  122.9 9.3 %collective-permute-done.34.refs_3_ = bf16[256,768]{1,0:T(8,128)(2,1)S(1)} collective-permute-done((bf16[256,768]{1,0:T(8,128)(2,1)S(1)}, bf16[256,768]{1,0:T(8,128)(2,1)S(1)}, u32[]{:S(2)}, u32[]{:S(2)}) %collective-permute-start.34) | collective-permute-done | bytes 393248 | tf_op jit(solution)/shard_map/ppermute | solution.py:918
  132.2 1.7 collective-permute-done.35.refs_4_
  134.0 4.5 %mixed_back.1 = (bf16[1024,192]{1,0:T(8,128)(2,1)S(1)}, bf16[768,192]{1,0:T(8,128)(2,1)S(1)}) custom-call(s32[9]{0:T(128)S(1)} %dynamic-slice_bitcast_fusion.scal.refs_0_, bf16[256,768]{1,0:T(8,128)(2,1)S(1)} %get-tuple-element.177.refs_1_, bf16[256,768]{1,0:T(8,128)(2,1)S(1)} %collective-permute-done.31.refs_2_, ...), custom_call_target="tpu_custom_call" | custom-call | bytes 9000000 | tf_op jit(solution)/shard_map/mixed_back/pallas_call | solution.py:148
  138.4 19.0 %attend_back.1 = (bf16[1024,192]{1,0:T(8,128)(2,1)S(1)}, bf16[1024,192]{1,0:T(8,128)(2,1)S(1)}, bf16[1024,192]{1,0:T(8,128)(2,1)S(1)}, f32[256,768]{1,0:T(8,128)...) custom-call(s32[9]{0:T(128)S(1)} %dynamic-slice_bitcast_fusion.scal.refs_0_, bf16[1024,192]{1,0:T(8,128)(2,1)} %get-tuple-element.184.refs_1_, ...), custom_call_target="tpu_custom_call" | custom-call | bytes 57600000 | tf_op jit(solution)/shard_map/attend_back/pallas_call | solution.py:148
  157.5 7.7 %project_back.1 = (bf16[768,896]{1,0:T(8,128)(2,1)S(1)}, f32[2,256,768]{2,1,0:T(8,128)S(1)}, bf16[2,256,768]{2,1,0:T(8,128)(2,1)S(1)}) custom-call(s32[9]{0:T(128)S(1)} %dynamic-slice_bitcast_fusion.scal.refs_0_, bf16[1024,768]{1,0:T(8,128)(2,1)} %get-tuple-element.183.refs_1_, bf16[1024,192]{1,0:T(8,128)(2,1)S(1)} %get-tuple-element.201.refs_2_, ...), custom_call_target="tpu_custom_call" | custom-call | bytes 18000000 | tf_op jit(solution)/shard_map/project_back/pallas_call | solution.py:148
  165.2 1.1 copy-done.3
  166.3 0.9 copy-done.8
  167.1 8.5 %all-to-all-done.1.refs_1_ = bf16[8,96,1536]{2,1,0:T(8,128)(2,1)} async-done(((bf16[8,96,1536]{2,1,0:T(8,128)(2,1)}), bf16[8,96,1536]{2,1,0:T(8,128)(2,1)}, u32[]{:S(2)}, u32[]{:S(2)}) %all-to-all-start.1) | async-done | bytes 2359328 | tf_op jit(solution)/shard_map/all_to_all | solution.py:988
  175.6 3.6 %all-to-all-start = ((bf16[8,96,896]{2,1,0:T(8,128)(2,1)}), bf16[8,96,896]{2,1,0:T(8,128)(2,1)S(1)}, u32[]{:S(2)}, u32[]{:S(2)}) async-start(bf16[8,96,896]{2,1,0:T(8,128)(2,1)} %bitcast.4), calls=%async_computation | async-start | bytes 2752512 | tf_op jit(solution)/shard_map/all_to_all | solution.py:988
  179.8 3.1 %owned_sum.1 = (bf16[96,1536]{1,0:T(8,128)(2,1)S(1)}, f32[8,128]{1,0:T(8,128)S(1)}) custom-call(s32[9]{0:T(128)S(1)} %dynamic-slice_bitcast_fusion.scal.refs_0_, bf16[8,96,1536]{2,1,0:T(8,128)(2,1)} %all-to-all-done.1.refs_1_), custom_call_target="tpu_custom_call" | custom-call | bytes 5400000 | tf_op jit(solution)/shard_map/owned_sum/pallas_call | solution.py:148
  182.9 1.6 collective-permute-start.39
  184.5 2.1 merge.4
  187.9 1.6 collective-permute-start.37
  189.5 3.4 %collective-permute-done.39.refs_2_ = bf16[96,1536]{1,0:T(8,128)(2,1)S(1)} collective-permute-done((bf16[96,1536]{1,0:T(8,128)(2,1)S(1)}, bf16[96,1536]{1,0:T(8,128)(2,1)S(1)}, u32[]{:S(2)}, u32[]{:S(2)}) %collective-permute-start.39) | collective-permute-done | bytes 294944 | tf_op jit(solution)/shard_map/ppermute | solution.py:918
  192.9 1.5 collective-permute-start.42
  194.4 6.9 %collective-permute-done.33.refs_2_ = bf16[256,768]{1,0:T(8,128)(2,1)S(1)} collective-permute-done((bf16[256,768]{1,0:T(8,128)(2,1)S(1)}, bf16[256,768]{1,0:T(8,128)(2,1)S(1)}, u32[]{:S(2)}, u32[]{:S(2)}) %collective-permute-start.33) | collective-permute-done | bytes 393248 | tf_op jit(solution)/shard_map/ppermute | solution.py:918
  201.3 7.6 %collective-permute-done.42.refs_7_ = f32[8,128]{1,0:T(8,128)S(1)} collective-permute-done((f32[8,128]{1,0:T(8,128)S(1)}, f32[8,128]{1,0:T(8,128)S(1)}, u32[]{:S(2)}, u32[]{:S(2)}) %collective-permute-start.42) | collective-permute-done | bytes 4128 | tf_op jit(solution)/shard_map/ppermute | solution.py:918
  208.9 2.6 %output_sum.1 = bf16[256,768]{1,0:T(8,128)(2,1)} custom-call(s32[9]{0:T(128)S(1)} %dynamic-slice_bitcast_fusion.scal.refs_0_, f32[256,768]{1,0:T(8,128)S(1)} %get-tuple-element.179.refs_1_, bf16[256,768]{1,0:T(8,128)(2,1)S(1)} %collective-permute-done.33.refs_2_, f32[256,768]{1,0:T(8,128)} %get-tuple-element.181.refs_3_, ...), custom_call_target="tpu_custom_call" | custom-call | bytes 2880000 | tf_op jit(solution)/shard_map/output_sum/pallas_call | solution.py:148
  211.5 3.2 %input_back.1 = f32[256,768]{1,0:T(8,128)} custom-call(s32[9]{0:T(128)S(1)} %dynamic-slice_bitcast_fusion.scal.refs_0_, f32[256,768]{1,0:T(8,128)S(1)} %get-tuple-element.212.refs_1_, bf16[256,768]{1,0:T(8,128)(2,1)S(1)} %collective-permute-done.37.refs_2_, bf16[256,768]{1,0:T(8,128)(2,1)} %refs_3_.3, f32[256,768]{1,0:T(8,128)} %get-tuple-element.214.refs_4_, ...), custom_call_target="tpu_custom_call" | custom-call | bytes 3600000 | tf_op jit(solution)/shard_map/input_back/pallas_call | solution.py:148
  214.8 0.7 owned_vector.1.refs_1_
  215.5 1.6 collective-permute-start.45
  217.4 5.5 %collective-permute-done.45.refs_3_ = bf16[96,1024]{1,0:T(8,128)(2,1)S(1)} collective-permute-done((bf16[96,1024]{1,0:T(8,128)(2,1)S(1)}, bf16[96,1024]{1,0:T(8,128)(2,1)S(1)}, u32[]{:S(2)}, u32[]{:S(2)}) %collective-permute-start.45) | collective-permute-done | bytes 196640 | tf_op jit(solution)/shard_map/ppermute | solution.py:918
  222.9 1.4 collective-permute-done.46.refs_4_
  224.4 1.2 join.1
  225.6 12.4 %all_to_all.15.total_ref = f32[8,8,128]{2,1,0:T(8,128)S(1)} all-to-all(f32[8,8,128]{2,1,0:T(8,128)S(1)} %broadcast_in_dim.3), channel_id=1, replica_groups=mesh['dp'=8,'head'=4] {'dp'}, dimensions={0} | all-to-all | bytes 65536 | tf_op jit(solution)/shard_map/all_to_all | solution.py:1132
  239.3 12.6 %adam.1 = (f32[96,3072]{1,0:T(8,128)}, f32[96,6144]{1,0:T(8,128)}, f32[12,96]{1,0:T(8,128)}, f32[96,3072]{1,0:T(8,128)}, f32[96,6144]{1,0:T(8,128)}, /*index=5*/...) custom-call(s32[9]{0:T(128)S(1)} %dynamic-slice_bitcast_fusion.scal., ...), custom_call_target="tpu_custom_call" | custom-call | bytes 32400000 | tf_op jit(solution)/shard_map/adam/pallas_call | solution.py:888
  (78 shorter events, 13.4 us)
Async XLA Ops:
  1.4 1.3 copy-start
  2.6 0.7 copy-start.6
  3.3 4.0 %copy-start.2 = (bf16[256,768]{1,0:T(8,128)(2,1)S(1)}, bf16[256,768]{1,0:T(8,128)(2,1)}, u32[]{:S(2)}) copy-start(bf16[256,768]{1,0:T(8,128)(2,1)} %refs_3_.3) | copy-start | bytes 1179652
  3.3 23.1 %copy-start.1 = (f32[96,6144]{1,0:T(8,128)S(1)}, f32[96,6144]{1,0:T(8,128)}, u32[]{:S(2)}) copy-start(f32[96,6144]{1,0:T(8,128)} %refs_8_.1) | copy-start | bytes 7077892
  4.2 7.5 %collective-permute-start.1 = (bf16[96,896]{1,0:T(8,128)(2,1)S(1)}, bf16[96,896]{1,0:T(8,128)(2,1)S(1)}, u32[]{:S(2)}, u32[]{:S(2)}) collective-permute-start(bf16[96,896]{1,0:T(8,128)(2,1)S(1)} %pack_attention.1.refs_3_), channel_id=1, source_target_pairs={{8,0},{16,8},{24,16},{28,24},{20,28},{12,20},{4,12},{0,4},{9,1},{1... | collective-permute-start | bytes 516104 | tf_op jit(solution)/shard_map/ppermute | solution.py:976
  7.2 5.8 %collective-permute-start = (bf16[96,896]{1,0:T(8,128)(2,1)S(1)}, bf16[96,896]{1,0:T(8,128)(2,1)S(1)}, u32[]{:S(2)}, u32[]{:S(2)}) collective-permute-start(bf16[96,896]{1,0:T(8,128)(2,1)S(1)} %pack_attention.1.refs_3_), channel_id=1, source_target_pairs={{0,8},{8,16},{16,24},{24,28},{28,20},{20,12},{12,4},{4,0},{1,9},{9... | collective-permute-start | bytes 516104 | tf_op jit(solution)/shard_map/ppermute | solution.py:973
  7.4 16.9 %collective-permute-start.6 = (bf16[256,768]{1,0:T(8,128)(2,1)S(1)}, bf16[256,768]{1,0:T(8,128)(2,1)S(1)}, u32[]{:S(2)}, u32[]{:S(2)}) collective-permute-start(bf16[256,768]{1,0:T(8,128)(2,1)S(1)} %copy-done.2), channel_id=1, source_target_pairs={{0,2},{1,3},{2,0},{3,1},{4,6},{5,7},{6,4},{7,5},{8,10},{9,11},{10,... | collective-permute-start | bytes 1179656 | tf_op jit(solution)/shard_map/ppermute | solution.py:918
  13.0 5.4 %collective-permute-start.2 = (bf16[96,896]{1,0:T(8,128)(2,1)S(1)}, bf16[96,896]{1,0:T(8,128)(2,1)S(1)}, u32[]{:S(2)}, u32[]{:S(2)}) collective-permute-start(bf16[96,896]{1,0:T(8,128)(2,1)S(1)} %collective-permute-done.refs_4_), channel_id=1, source_target_pairs={{0,8},{8,16},{16,24},{24,28},{28,20},{20,12},{12,4},{4,0},{1,9},{9... | collective-permute-start | bytes 516104 | tf_op jit(solution)/shard_map/ppermute | solution.py:973
  13.5 5.4 %collective-permute-start.3 = (bf16[96,896]{1,0:T(8,128)(2,1)S(1)}, bf16[96,896]{1,0:T(8,128)(2,1)S(1)}, u32[]{:S(2)}, u32[]{:S(2)}) collective-permute-start(bf16[96,896]{1,0:T(8,128)(2,1)S(1)} %collective-permute-done.1.refs_5_), channel_id=1, source_target_pairs={{8,0},{16,8},{24,16},{28,24},{20,28},{12,20},{4,12},{0,4},{9,1},{1... | collective-permute-start | bytes 516104 | tf_op jit(solution)/shard_map/ppermute | solution.py:976
  18.9 5.4 %collective-permute-start.4 = (bf16[96,896]{1,0:T(8,128)(2,1)S(1)}, bf16[96,896]{1,0:T(8,128)(2,1)S(1)}, u32[]{:S(2)}, u32[]{:S(2)}) collective-permute-start(bf16[96,896]{1,0:T(8,128)(2,1)S(1)} %collective-permute-done.3.refs_7_), channel_id=1, source_target_pairs={{8,0},{16,8},{24,16},{28,24},{20,28},{12,20},{4,12},{0,4},{9,1},{1... | collective-permute-start | bytes 516104 | tf_op jit(solution)/shard_map/ppermute | solution.py:976
  24.3 9.4 %collective-permute-start.5 = (bf16[256,768]{1,0:T(8,128)(2,1)S(1)}, bf16[256,768]{1,0:T(8,128)(2,1)S(1)}, u32[]{:S(2)}, u32[]{:S(2)}) collective-permute-start(bf16[256,768]{1,0:T(8,128)(2,1)S(1)} %copy-done.2), channel_id=1, source_target_pairs={{0,1},{1,0},{2,3},{3,2},{4,5},{5,4},{6,7},{7,6},{8,9},{9,8},{10,11... | collective-permute-start | bytes 1179656 | tf_op jit(solution)/shard_map/ppermute | solution.py:918
  24.3 9.4 %collective-permute-start.7 = (bf16[256,768]{1,0:T(8,128)(2,1)S(1)}, bf16[256,768]{1,0:T(8,128)(2,1)S(1)}, u32[]{:S(2)}, u32[]{:S(2)}) collective-permute-start(bf16[256,768]{1,0:T(8,128)(2,1)S(1)} %collective-permute-done.6.refs_3_), channel_id=1, source_target_pairs={{0,1},{1,0},{2,3},{3,2},{4,5},{5,4},{6,7},{7,6},{8,9},{9,8},{10,11... | collective-permute-start | bytes 1179656 | tf_op jit(solution)/shard_map/ppermute | solution.py:918
  24.8 7.2 %collective-permute-start.9 = (bf16[96,896]{1,0:T(8,128)(2,1)S(1)}, bf16[96,896]{1,0:T(8,128)(2,1)S(1)}, u32[]{:S(2)}, u32[]{:S(2)}) collective-permute-start(bf16[96,896]{1,0:T(8,128)(2,1)S(1)} %collective-permute-done.2.refs_6_), channel_id=1, source_target_pairs={{0,8},{8,16},{16,24},{24,28},{28,20},{20,12},{12,4},{4,0},{1,9},{9... | collective-permute-start | bytes 516104 | tf_op jit(solution)/shard_map/ppermute | solution.py:973
  27.2 13.9 %copy-start.5 = (s32[1,1024]{1,0:T(1,128)S(1)}, s32[1,1024]{1,0:T(1,128)}, u32[]{:S(2)}) copy-start(s32[1,1024]{1,0:T(1,128)} %refs_5_.2) | copy-start | bytes 12292
  27.2 19.5 %collective-permute-start.22 = (bf16[96,1536]{1,0:T(8,128)(2,1)S(1)}, bf16[96,1536]{1,0:T(8,128)(2,1)S(1)}, u32[]{:S(2)}, u32[]{:S(2)}) collective-permute-start(bf16[96,1536]{1,0:T(8,128)(2,1)S(1)} %pack_forward.1.refs_15_), channel_id=1, source_target_pairs={{0,8},{8,16},{16,24},{24,28},{28,20},{20,12},{12,4},{4,0},{1,9},{9... | collective-permute-start | bytes 884744 | tf_op jit(solution)/shard_map/ppermute | solution.py:973
  28.9 17.8 %collective-permute-start.23 = (bf16[96,1536]{1,0:T(8,128)(2,1)S(1)}, bf16[96,1536]{1,0:T(8,128)(2,1)S(1)}, u32[]{:S(2)}, u32[]{:S(2)}) collective-permute-start(bf16[96,1536]{1,0:T(8,128)(2,1)S(1)} %pack_forward.1.refs_15_), channel_id=1, source_target_pairs={{8,0},{16,8},{24,16},{28,24},{20,28},{12,20},{4,12},{0,4},{9,1},{1... | collective-permute-start | bytes 884744 | tf_op jit(solution)/shard_map/ppermute | solution.py:976
  32.0 9.0 %collective-permute-start.10 = (bf16[96,896]{1,0:T(8,128)(2,1)S(1)}, bf16[96,896]{1,0:T(8,128)(2,1)S(1)}, u32[]{:S(2)}, u32[]{:S(2)}) collective-permute-start(bf16[96,896]{1,0:T(8,128)(2,1)S(1)} %collective-permute-done.9.refs_8_), channel_id=1, source_target_pairs={{0,8},{8,16},{16,24},{24,28},{28,20},{20,12},{12,4},{4,0},{1,9},{9... | collective-permute-start | bytes 516104 | tf_op jit(solution)/shard_map/ppermute | solution.py:973
  34.4 14.3 %copy-start.4 = (bf16[256,768]{1,0:T(8,128)(2,1)S(1)}, bf16[256,768]{1,0:T(8,128)(2,1)}, u32[]{:S(2)}) copy-start(bf16[256,768]{1,0:T(8,128)(2,1)} %refs_1_.6) | copy-start | bytes 1179652
  45.0 12.1 %collective-permute-start.11 = (bf16[768,192]{1,0:T(8,128)(2,1)S(1)}, bf16[768,192]{1,0:T(8,128)(2,1)S(1)}, u32[]{:S(2)}, u32[]{:S(2)}) collective-permute-start(bf16[768,192]{1,0:T(8,128)(2,1)S(1)} %get-tuple-element.153.refs_11_), channel_id=1, source_target_pairs={{0,2},{1,3},{2,0},{3,1},{4,6},{5,7},{6,4},{7,5},{8,10},{9,11},{10,... | collective-permute-start | bytes 884744 | tf_op jit(solution)/shard_map/ppermute | solution.py:918
  46.7 16.3 %collective-permute-start.24 = (bf16[96,1536]{1,0:T(8,128)(2,1)S(1)}, bf16[96,1536]{1,0:T(8,128)(2,1)S(1)}, u32[]{:S(2)}, u32[]{:S(2)}) collective-permute-start(bf16[96,1536]{1,0:T(8,128)(2,1)S(1)} %collective-permute-done.22.refs_16_), channel_id=1, source_target_pairs={{0,8},{8,16},{16,24},{24,28},{28,20},{20,12},{12,4},{4,0},{1,9},{9... | collective-permute-start | bytes 884744 | tf_op jit(solution)/shard_map/ppermute | solution.py:973
  48.3 14.8 %collective-permute-start.25 = (bf16[96,1536]{1,0:T(8,128)(2,1)S(1)}, bf16[96,1536]{1,0:T(8,128)(2,1)S(1)}, u32[]{:S(2)}, u32[]{:S(2)}) collective-permute-start(bf16[96,1536]{1,0:T(8,128)(2,1)S(1)} %collective-permute-done.23.refs_17_), channel_id=1, source_target_pairs={{8,0},{16,8},{24,16},{28,24},{20,28},{12,20},{4,12},{0,4},{9,1},{1... | collective-permute-start | bytes 884744 | tf_op jit(solution)/shard_map/ppermute | solution.py:976
  48.7 16.8 %collective-permute-start.8 = (bf16[256,768]{1,0:T(8,128)(2,1)S(1)}, bf16[256,768]{1,0:T(8,128)(2,1)S(1)}, u32[]{:S(2)}, u32[]{:S(2)}) collective-permute-start(bf16[256,768]{1,0:T(8,128)(2,1)S(1)} %copy-done.4), channel_id=1, source_target_pairs={{0,2},{1,3},{2,0},{3,1},{4,6},{5,7},{6,4},{7,5},{8,10},{9,11},{10,... | collective-permute-start | bytes 1179656 | tf_op jit(solution)/shard_map/ppermute | solution.py:918
  53.5 17.7 %collective-permute-start.12 = (bf16[512,192]{1,0:T(8,128)(2,1)S(1)}, bf16[512,192]{1,0:T(8,128)(2,1)S(1)}, u32[]{:S(2)}, u32[]{:S(2)}) collective-permute-start(bf16[512,192]{1,0:T(8,128)(2,1)S(1)} %get-tuple-element.151.refs_3_.refs_9_), channel_id=1, source_target_pairs={{0,2},{1,3},{2,0},{3,1},{4,6},{5,7},{6,4},{7,5},{8,10},{9,11},{10,... | collective-permute-start | bytes 589832 | tf_op jit(solution)/shard_map/ppermute | solution.py:918
  61.3 13.6 %collective-permute-start.13 = (bf16[512,192]{1,0:T(8,128)(2,1)S(1)}, bf16[512,192]{1,0:T(8,128)(2,1)S(1)}, u32[]{:S(2)}, u32[]{:S(2)}) collective-permute-start(bf16[512,192]{1,0:T(8,128)(2,1)S(1)} %attend.3.refs_4_.refs_10_), channel_id=1, source_target_pairs={{0,2},{1,3},{2,0},{3,1},{4,6},{5,7},{6,4},{7,5},{8,10},{9,11},{10,... | collective-permute-start | bytes 589832 | tf_op jit(solution)/shard_map/ppermute | solution.py:918
  63.0 12.4 %collective-permute-start.26 = (bf16[96,1536]{1,0:T(8,128)(2,1)S(1)}, bf16[96,1536]{1,0:T(8,128)(2,1)S(1)}, u32[]{:S(2)}, u32[]{:S(2)}) collective-permute-start(bf16[96,1536]{1,0:T(8,128)(2,1)S(1)} %collective-permute-done.24.refs_18_), channel_id=1, source_target_pairs={{0,8},{8,16},{16,24},{24,28},{28,20},{20,12},{12,4},{4,0},{1,9},{9... | collective-permute-start | bytes 884744 | tf_op jit(solution)/shard_map/ppermute | solution.py:973
  64.6 11.3 %collective-permute-start.27 = (bf16[96,1536]{1,0:T(8,128)(2,1)S(1)}, bf16[96,1536]{1,0:T(8,128)(2,1)S(1)}, u32[]{:S(2)}, u32[]{:S(2)}) collective-permute-start(bf16[96,1536]{1,0:T(8,128)(2,1)S(1)} %collective-permute-done.25.refs_19_), channel_id=1, source_target_pairs={{8,0},{16,8},{24,16},{28,24},{20,28},{12,20},{4,12},{0,4},{9,1},{1... | collective-permute-start | bytes 884744 | tf_op jit(solution)/shard_map/ppermute | solution.py:976
  74.9 4.7 %collective-permute-start.14 = (bf16[256,768]{1,0:T(8,128)(2,1)S(1)}, bf16[256,768]{1,0:T(8,128)(2,1)S(1)}, u32[]{:S(2)}, u32[]{:S(2)}) collective-permute-start(bf16[256,768]{1,0:T(8,128)(2,1)S(1)} %copy-done.4), channel_id=1, source_target_pairs={{0,1},{1,0},{2,3},{3,2},{4,5},{5,4},{6,7},{7,6},{8,9},{9,8},{10,11... | collective-permute-start | bytes 1179656 | tf_op jit(solution)/shard_map/ppermute | solution.py:918
  74.9 4.7 %collective-permute-start.15 = (bf16[256,768]{1,0:T(8,128)(2,1)S(1)}, bf16[256,768]{1,0:T(8,128)(2,1)S(1)}, u32[]{:S(2)}, u32[]{:S(2)}) collective-permute-start(bf16[256,768]{1,0:T(8,128)(2,1)S(1)} %collective-permute-done.8.refs_3_), channel_id=1, source_target_pairs={{0,1},{1,0},{2,3},{3,2},{4,5},{5,4},{6,7},{7,6},{8,9},{9,8},{10,11... | collective-permute-start | bytes 1179656 | tf_op jit(solution)/shard_map/ppermute | solution.py:918
  75.4 2.1 collective-permute-start.17
  75.4 2.5 collective-permute-start.19
  75.9 5.6 %collective-permute-start.20 = (bf16[768,192]{1,0:T(8,128)(2,1)S(1)}, bf16[768,192]{1,0:T(8,128)(2,1)S(1)}, u32[]{:S(2)}, u32[]{:S(2)}) collective-permute-start(bf16[768,192]{1,0:T(8,128)(2,1)S(1)} %get-tuple-element.153.refs_11_), channel_id=1, source_target_pairs={{0,1},{1,0},{2,3},{3,2},{4,5},{5,4},{6,7},{7,6},{8,9},{9,8},{10,11... | collective-permute-start | bytes 884744 | tf_op jit(solution)/shard_map/ppermute | solution.py:918
  77.6 4.0 %collective-permute-start.21 = (bf16[768,192]{1,0:T(8,128)(2,1)S(1)}, bf16[768,192]{1,0:T(8,128)(2,1)S(1)}, u32[]{:S(2)}, u32[]{:S(2)}) collective-permute-start(bf16[768,192]{1,0:T(8,128)(2,1)S(1)} %collective-permute-done.11.refs_13_), channel_id=1, source_target_pairs={{0,1},{1,0},{2,3},{3,2},{4,5},{5,4},{6,7},{7,6},{8,9},{9,8},{10,11... | collective-permute-start | bytes 884744 | tf_op jit(solution)/shard_map/ppermute | solution.py:918
  77.9 9.1 %collective-permute-start.28 = (bf16[96,1536]{1,0:T(8,128)(2,1)S(1)}, bf16[96,1536]{1,0:T(8,128)(2,1)S(1)}, u32[]{:S(2)}, u32[]{:S(2)}) collective-permute-start(bf16[96,1536]{1,0:T(8,128)(2,1)S(1)} %collective-permute-done.26.refs_20_), channel_id=1, source_target_pairs={{0,8},{8,16},{16,24},{24,28},{28,20},{20,12},{12,4},{4,0},{1,9},{9... | collective-permute-start | bytes 884744 | tf_op jit(solution)/shard_map/ppermute | solution.py:973
  79.6 1.5 collective-permute-start.16
  79.6 1.9 collective-permute-start.18
  98.2 2.4 collective-permute-start.29
  101.3 11.2 %collective-permute-start.30 = (bf16[256,768]{1,0:T(8,128)(2,1)S(1)}, bf16[256,768]{1,0:T(8,128)(2,1)S(1)}, u32[]{:S(2)}, u32[]{:S(2)}) collective-permute-start(bf16[256,768]{1,0:T(8,128)(2,1)S(1)} %get-tuple-element.165), channel_id=1, source_target_pairs={{0,2},{1,3},{2,0},{3,1},{4,6},{5,7},{6,4},{7,5},{8,10},{9,11},{10,... | collective-permute-start | bytes 1179656 | tf_op jit(solution)/shard_map/ppermute | solution.py:918
  110.5 5.0 %copy-start.7 = (bf16[2,256,768]{2,1,0:T(8,128)(2,1)}, bf16[2,256,768]{2,1,0:T(8,128)(2,1)S(1)}, u32[]{:S(2)}) copy-start(bf16[2,256,768]{2,1,0:T(8,128)(2,1)S(1)} %get-tuple-element.178) | copy-start | bytes 2359300
  113.7 1.8 collective-permute-start.31
  115.5 60.1 %all-to-all-start.1 = ((bf16[8,96,1536]{2,1,0:T(8,128)(2,1)}), bf16[8,96,1536]{2,1,0:T(8,128)(2,1)}, u32[]{:S(2)}, u32[]{:S(2)}) async-start(bf16[8,96,1536]{2,1,0:T(8,128)(2,1)} %bitcast.2), calls=%async_computation.1 | async-start | bytes 4718592 | tf_op jit(solution)/shard_map/all_to_all | solution.py:988
  121.4 10.9 %collective-permute-start.34 = (bf16[256,768]{1,0:T(8,128)(2,1)S(1)}, bf16[256,768]{1,0:T(8,128)(2,1)S(1)}, u32[]{:S(2)}, u32[]{:S(2)}) collective-permute-start(bf16[256,768]{1,0:T(8,128)(2,1)S(1)} %get-tuple-element.177.refs_1_), channel_id=1, source_target_pairs={{0,2},{1,3},{2,0},{3,1},{4,6},{5,7},{6,4},{7,5},{8,10},{9,11},{10,... | collective-permute-start | bytes 1179656 | tf_op jit(solution)/shard_map/ppermute | solution.py:918
  132.2 1.7 collective-permute-start.35
  165.2 1.1 copy-start.3
  166.3 0.9 copy-start.8
  175.6 39.1 %all-to-all-start = ((bf16[8,96,896]{2,1,0:T(8,128)(2,1)}), bf16[8,96,896]{2,1,0:T(8,128)(2,1)S(1)}, u32[]{:S(2)}, u32[]{:S(2)}) async-start(bf16[8,96,896]{2,1,0:T(8,128)(2,1)} %bitcast.4), calls=%async_computation | async-start | bytes 2752512 | tf_op jit(solution)/shard_map/all_to_all | solution.py:988
  179.3 5.3 %collective-permute-start.32 = (bf16[2,256,768]{2,1,0:T(8,128)(2,1)}, bf16[2,256,768]{2,1,0:T(8,128)(2,1)S(1)}, u32[]{:S(2)}, u32[]{:S(2)}) collective-permute-start(bf16[2,256,768]{2,1,0:T(8,128)(2,1)} %copy-done.7), channel_id=1, source_target_pairs={{0,1},{1,0},{2,3},{3,2},{4,5},{5,4},{6,7},{7,6},{8,9},{9,8},{10,11... | collective-permute-start | bytes 2359304 | tf_op jit(solution)/shard_map/ppermute | solution.py:918
  179.3 7.9 %collective-permute-start.36 = (bf16[2,256,768]{2,1,0:T(8,128)(2,1)}, bf16[2,256,768]{2,1,0:T(8,128)(2,1)S(1)}, u32[]{:S(2)}, u32[]{:S(2)}) collective-permute-start(bf16[2,256,768]{2,1,0:T(8,128)(2,1)} %copy-done.8), channel_id=1, source_target_pairs={{0,1},{1,0},{2,3},{3,2},{4,5},{5,4},{6,7},{7,6},{8,9},{9,8},{10,11... | collective-permute-start | bytes 2359304 | tf_op jit(solution)/shard_map/ppermute | solution.py:918
  182.9 9.9 %collective-permute-start.39 = (bf16[96,1536]{1,0:T(8,128)(2,1)S(1)}, bf16[96,1536]{1,0:T(8,128)(2,1)S(1)}, u32[]{:S(2)}, u32[]{:S(2)}) collective-permute-start(bf16[96,1536]{1,0:T(8,128)(2,1)S(1)} %get-tuple-element.219.refs_0_), channel_id=1, source_target_pairs={{0,2},{1,3},{2,0},{3,1},{4,6},{5,7},{6,4},{7,5},{8,10},{9,11},{10,... | collective-permute-start | bytes 884744 | tf_op jit(solution)/shard_map/ppermute | solution.py:918
  186.6 14.6 %collective-permute-start.33 = (bf16[256,768]{1,0:T(8,128)(2,1)S(1)}, bf16[256,768]{1,0:T(8,128)(2,1)S(1)}, u32[]{:S(2)}, u32[]{:S(2)}) collective-permute-start(bf16[256,768]{1,0:T(8,128)(2,1)S(1)} %get-tuple-element.180), channel_id=1, source_target_pairs={{0,2},{1,3},{2,0},{3,1},{4,6},{5,7},{6,4},{7,5},{8,10},{9,11},{10,... | collective-permute-start | bytes 1179656 | tf_op jit(solution)/shard_map/ppermute | solution.py:918
  187.9 23.7 %collective-permute-start.37 = (bf16[256,768]{1,0:T(8,128)(2,1)S(1)}, bf16[256,768]{1,0:T(8,128)(2,1)S(1)}, u32[]{:S(2)}, u32[]{:S(2)}) collective-permute-start(bf16[256,768]{1,0:T(8,128)(2,1)S(1)} %get-tuple-element.213), channel_id=1, source_target_pairs={{0,2},{1,3},{2,0},{3,1},{4,6},{5,7},{6,4},{7,5},{8,10},{9,11},{10,... | collective-permute-start | bytes 1179656 | tf_op jit(solution)/shard_map/ppermute | solution.py:918
  189.5 25.3 %collective-permute-start.38 = (bf16[96,1536]{1,0:T(8,128)(2,1)S(1)}, bf16[96,1536]{1,0:T(8,128)(2,1)S(1)}, u32[]{:S(2)}, u32[]{:S(2)}) collective-permute-start(bf16[96,1536]{1,0:T(8,128)(2,1)S(1)} %get-tuple-element.219.refs_0_), channel_id=1, source_target_pairs={{0,1},{1,0},{2,3},{3,2},{4,5},{5,4},{6,7},{7,6},{8,9},{9,8},{10,11... | collective-permute-start | bytes 884744 | tf_op jit(solution)/shard_map/ppermute | solution.py:918
  192.9 21.9 %collective-permute-start.40 = (bf16[96,1536]{1,0:T(8,128)(2,1)S(1)}, bf16[96,1536]{1,0:T(8,128)(2,1)S(1)}, u32[]{:S(2)}, u32[]{:S(2)}) collective-permute-start(bf16[96,1536]{1,0:T(8,128)(2,1)S(1)} %collective-permute-done.39.refs_2_), channel_id=1, source_target_pairs={{0,1},{1,0},{2,3},{3,2},{4,5},{5,4},{6,7},{7,6},{8,9},{9,8},{10,11... | collective-permute-start | bytes 884744 | tf_op jit(solution)/shard_map/ppermute | solution.py:918
  192.9 16.1 %collective-permute-start.42 = (f32[8,128]{1,0:T(8,128)S(1)}, f32[8,128]{1,0:T(8,128)S(1)}, u32[]{:S(2)}, u32[]{:S(2)}) collective-permute-start(f32[8,128]{1,0:T(8,128)S(1)} %get-tuple-element.220.refs_5_), channel_id=1, source_target_pairs={{0,2},{1,3},{2,0},{3,1},{4,6},{5,7},{6,4},{7,5},{8,10},{9,11},{10,... | collective-permute-start | bytes 12296 | tf_op jit(solution)/shard_map/ppermute | solution.py:918
  201.3 13.5 %collective-permute-start.41 = (f32[8,128]{1,0:T(8,128)S(1)}, f32[8,128]{1,0:T(8,128)S(1)}, u32[]{:S(2)}, u32[]{:S(2)}) collective-permute-start(f32[8,128]{1,0:T(8,128)S(1)} %get-tuple-element.220.refs_5_), channel_id=1, source_target_pairs={{0,1},{1,0},{2,3},{3,2},{4,5},{5,4},{6,7},{7,6},{8,9},{9,8},{10,11... | collective-permute-start | bytes 12296 | tf_op jit(solution)/shard_map/ppermute | solution.py:918
  208.9 5.8 %collective-permute-start.43 = (f32[8,128]{1,0:T(8,128)S(1)}, f32[8,128]{1,0:T(8,128)S(1)}, u32[]{:S(2)}, u32[]{:S(2)}) collective-permute-start(f32[8,128]{1,0:T(8,128)S(1)} %collective-permute-done.42.refs_7_), channel_id=1, source_target_pairs={{0,1},{1,0},{2,3},{3,2},{4,5},{5,4},{6,7},{7,6},{8,9},{9,8},{10,11... | collective-permute-start | bytes 12296 | tf_op jit(solution)/shard_map/ppermute | solution.py:918
  215.5 7.4 %collective-permute-start.45 = (bf16[96,1024]{1,0:T(8,128)(2,1)S(1)}, bf16[96,1024]{1,0:T(8,128)(2,1)S(1)}, u32[]{:S(2)}, u32[]{:S(2)}) collective-permute-start(bf16[96,1024]{1,0:T(8,128)(2,1)S(1)} %owned_vector.1.refs_1_), channel_id=1, source_target_pairs={{0,2},{1,3},{2,0},{3,1},{4,6},{5,7},{6,4},{7,5},{8,10},{9,11},{10,... | collective-permute-start | bytes 589832 | tf_op jit(solution)/shard_map/ppermute | solution.py:918
  217.1 5.8 %collective-permute-start.44 = (bf16[96,1024]{1,0:T(8,128)(2,1)S(1)}, bf16[96,1024]{1,0:T(8,128)(2,1)S(1)}, u32[]{:S(2)}, u32[]{:S(2)}) collective-permute-start(bf16[96,1024]{1,0:T(8,128)(2,1)S(1)} %owned_vector.1.refs_1_), channel_id=1, source_target_pairs={{0,1},{1,0},{2,3},{3,2},{4,5},{5,4},{6,7},{7,6},{8,9},{9,8},{10,11... | collective-permute-start | bytes 589832 | tf_op jit(solution)/shard_map/ppermute | solution.py:918
  222.9 1.4 collective-permute-start.46
